TPU v7x, 256 devices: a whole 4x4x8 slice. The times are simulated.
256 devices in a mesh: req: 64 (over x, z, core), tp: 4 (over y).
Axes of the slice: x: 4, y: 4, z: 8, core: 2. Of those that a mesh axis runs over, the one named last changes fastest.
Arguments:
- hidden_in: bfloat16 [512, 1600], P('req'), may hold values from -6 to 6
- norm_gain: float32 [1600], replicated, may hold values from 0.1 to 1.9
- query_weight: bfloat16 [1600, 1280], P(None, 'tp'), may hold values from -0.15625 to 0.15625
- memory_weight: bfloat16 [1600, 512], P(None, 'tp'), may hold values from -0.15625 to 0.15625
- attention_out: bfloat16 [1280, 1600], P('tp'), may hold values from -0.15625 to 0.15625
- attention_gain: float32 [1280], P('tp'), may hold values from 0.1 to 1.9
- mamba_input: bfloat16 [2, 1600, 1600], P(None, None, 'tp'), may hold values from -0.15625 to 0.15625
- conv_weight: float32 [4, 1600], P(None, 'tp'), may hold values from -3 to 3
- conv_state: bfloat16 [512, 3, 1600], P('req', None, 'tp'), may hold values from -6 to 6
- select_weight: bfloat16 [1600, 132], P('tp'), may hold values from -0.15625 to 0.15625
- step_weight: bfloat16 [100, 1600], P(None, 'tp'), may hold values from -0.625 to 0.625
- step_bias: float32 [1600], P('tp'), may hold values from -4 to -1
- decay_log: float32 [16, 1600], P(None, 'tp'), may hold values from 0 to 2.77
- skip_gain: float32 [1600], P('tp'), may hold values from 0.5 to 1.5
- scan_state: float32 [512, 16, 1600], P('req', None, 'tp'), may hold values from -6 to 6
- mamba_gain: float32 [1600], P('tp'), may hold values from 0.1 to 1.9
- mamba_out: bfloat16 [1600, 1600], P('tp'), may hold values from -0.15625 to 0.15625
- cache_blocks: bfloat16 [2176, 4, 512, 128], P('req', 'tp'), as said below
- lengths: int32 [512], replicated, may hold values from 257 to 8192, as said below
- slot_request: int32 [2176], P('req'), may hold values from -1 to 511, as said below
- slot_block: int32 [2176], P('req'), may hold values from 0 to 15, as said below
Outputs:
- layer_out: bfloat16 [512, 1600], P('req', 'tp')
- new_state: float32 [512, 16, 1600], P('req', None, 'tp')
Inputs may be any that keep to these rules, and one draw needn't show every extreme that they name: `lengths`: some request holds exactly 8192 tokens. `slot_request`: -1 marks an empty slot; a request with L cached tokens fills exactly ceil(L / 512) slots; the slots of one index of req hold at most 2 blocks of the requests of any one index of req (requests r with equal r // 8), and some index of req holds exactly 2. `slot_block`: the slots of one request carry its block numbers 0 to ceil(L / 512) - 1, each once; empty slots carry 0. `cache_blocks`: the first 64 entries of the last dimension are keys, the rest values.
All inputs are finite; a program needn't handle non-finite values.
Results may differ from a plain program's by a relative error of at most 0.012.
Values may be sent and summed in bfloat16 or wider, within the bound.
A program may use at most 64 MiB of HBM per device.

v0:
```python
import jax
import jax.numpy as jnp
from jax import lax
from jax.sharding import PartitionSpec as P

HQ = 20
HD = 64
MI = 1600


def rotate_pairs(vector, position):
    head_dim = vector.shape[-1]
    half_dim = head_dim // 2
    frequency = jnp.power(
        jnp.float32(10000.0), -jnp.arange(half_dim, dtype=jnp.float32) * (2.0 / head_dim)
    )
    angles = position.astype(jnp.float32)[:, None, None] * frequency
    cosine = jnp.cos(angles)
    sine_part = jnp.sin(angles)
    front_half = vector[..., :half_dim]
    back_half = vector[..., half_dim:]
    return jnp.concatenate(
        [front_half * cosine - back_half * sine_part, back_half * cosine + front_half * sine_part],
        -1,
    )


def body(
    hidden_in,
    norm_gain,
    query_weight,
    memory_weight,
    attention_out,
    attention_gain,
    mamba_input,
    conv_weight,
    conv_state,
    select_weight,
    step_weight,
    step_bias,
    decay_log,
    skip_gain,
    scan_state,
    mamba_gain,
    mamba_out,
    cache_blocks,
    lengths,
    slot_request,
    slot_block,
):
    row_count = hidden_in.shape[0]
    model_width = hidden_in.shape[1]
    head_dim = cache_blocks.shape[3] // 2
    head_count = query_weight.shape[1] // head_dim
    block_len = cache_blocks.shape[2]
    slot_count = cache_blocks.shape[0]
    request_count = lengths.shape[0]
    holders = lax.axis_size("req")
    tp_count = lax.axis_size("tp")
    own_first = lax.axis_index("req") * row_count
    own_len = lax.dynamic_slice_in_dim(lengths, own_first, row_count)
    hidden_f = hidden_in.astype(jnp.float32)
    normed = (
        hidden_f * lax.rsqrt(jnp.mean(hidden_f * hidden_f, -1, keepdims=True) + 1e-06) * norm_gain
    ).astype(jnp.bfloat16)
    query_raw = jnp.dot(normed, query_weight, preferred_element_type=jnp.float32).reshape(
        row_count, head_count, head_dim
    )
    query = rotate_pairs(query_raw, own_len).astype(jnp.bfloat16)
    memory = jnp.dot(normed, memory_weight, preferred_element_type=jnp.float32)
    key_new = rotate_pairs(memory[:, None, :head_dim], own_len).astype(jnp.bfloat16)
    value_new = memory[:, head_dim:].astype(jnp.bfloat16)
    all_query = lax.all_gather(
        query.reshape(row_count, head_count * head_dim), "req", axis=0, tiled=True
    )
    slot_used = slot_request >= 0
    owner_row = jnp.where(slot_used, slot_request, 0)
    slot_query = jnp.take(all_query, owner_row, axis=0).reshape(slot_count, head_count, head_dim)
    keys = cache_blocks[:, 0, :, :head_dim]
    values = cache_blocks[:, 0, :, head_dim:]
    valid_len = jnp.where(slot_used, jnp.take(lengths, owner_row) - slot_block * block_len, 0)
    live_mask = jnp.arange(block_len)[None, :] < valid_len[:, None]
    scores = jnp.einsum(
        "shd,std->sht", slot_query, keys, preferred_element_type=jnp.float32
    ) * head_dim ** (-0.5)
    scores = jnp.where(live_mask[:, None, :], scores, -1e30)
    block_max = jnp.max(scores, 2)
    weights = jnp.where(live_mask[:, None, :], jnp.exp(scores - block_max[..., None]), 0.0).astype(
        jnp.bfloat16
    )
    block_sum = jnp.sum(weights.astype(jnp.float32), 2)
    block_out = jnp.einsum("sht,std->shd", weights, values, preferred_element_type=jnp.float32)
    own_score = jnp.sum(query.astype(jnp.float32) * key_new.astype(jnp.float32), -1) * head_dim ** (
        -0.5
    )
    value_own = value_new.astype(jnp.float32)[:, None, :]
    owner_match = slot_request[:, None] == jnp.arange(request_count)[None, :]
    request_max = jnp.max(jnp.where(owner_match[:, :, None], block_max[:, None, :], -1e30), axis=0)
    owner_table = owner_match.astype(jnp.float32)
    rescale = jnp.exp(block_max - jnp.take(request_max, owner_row, axis=0))
    scaled_out = (block_out * rescale[..., None]).reshape(slot_count, head_count * head_dim)
    part_out = jnp.dot(owner_table.T, scaled_out, precision=lax.Precision.HIGHEST)
    part_sum = jnp.dot(owner_table.T, block_sum * rescale, precision=lax.Precision.HIGHEST)
    part_out, part_sum = (part_out, part_sum)
    got_out, got_sum, got_max = (
        lax.all_to_all(
            part_out.reshape(holders, row_count, head_count * head_dim),
            "req",
            split_axis=0,
            concat_axis=0,
            tiled=True,
        ),
        lax.all_to_all(
            part_sum.reshape(holders, row_count, head_count),
            "req",
            split_axis=0,
            concat_axis=0,
            tiled=True,
        ),
        lax.all_to_all(
            request_max.reshape(holders, row_count, head_count),
            "req",
            split_axis=0,
            concat_axis=0,
            tiled=True,
        ),
    )
    top = jnp.maximum(jnp.max(got_max, 0), own_score)
    source_weight = jnp.exp(got_max - top[None])
    numer = jnp.sum(
        got_out.reshape(holders, row_count, head_count, head_dim) * source_weight[..., None], 0
    )
    denom = jnp.sum(got_sum * source_weight, 0)
    own_weight = jnp.exp(own_score - top)
    numer = numer + own_weight[..., None] * value_own
    denom = denom + own_weight
    attention = (numer / denom[..., None]).reshape(row_count, head_count * head_dim)
    mamba_x = jnp.dot(normed, mamba_input[0], preferred_element_type=jnp.float32).astype(
        jnp.bfloat16
    )
    gate_branch = jnp.dot(normed, mamba_input[1], preferred_element_type=jnp.float32)
    taps = conv_weight.shape[0]
    conv_sum = conv_weight[taps - 1] * mamba_x.astype(jnp.float32)
    for tap_index in range(taps - 1):
        conv_sum = conv_sum + conv_weight[tap_index] * conv_state[:, tap_index].astype(jnp.float32)
    activated = jax.nn.silu(conv_sum).astype(jnp.bfloat16)
    selection = lax.psum(
        jnp.dot(activated, select_weight, preferred_element_type=jnp.float32), "tp"
    )
    rank_width = step_weight.shape[0]
    state_width = decay_log.shape[0]
    step_rank = selection[:, :rank_width].astype(jnp.bfloat16)
    input_map = selection[:, rank_width : rank_width + state_width]
    output_map = selection[:, rank_width + state_width :]
    step_size = jax.nn.softplus(
        jnp.dot(step_rank, step_weight, preferred_element_type=jnp.float32) + step_bias
    )
    active_f = activated.astype(jnp.float32)
    new_state = (
        jnp.exp(-step_size[:, None, :] * jnp.exp(decay_log)[None]) * scan_state
        + step_size[:, None, :] * input_map[:, :, None] * active_f[:, None, :]
    )
    mamba_y = (jnp.sum(output_map[:, :, None] * new_state, 1) + skip_gain * active_f) * jax.nn.silu(
        gate_branch
    )
    attn_square = jnp.sum(attention * attention, -1)
    mamba_square = jnp.sum(mamba_y * mamba_y, -1)
    attn_used = (attention * attention_gain).astype(jnp.bfloat16)
    mamba_used = (mamba_y * mamba_gain).astype(jnp.bfloat16)
    attn_proj = jnp.dot(attn_used, attention_out, preferred_element_type=jnp.float32)
    mamba_proj = jnp.dot(mamba_used, mamba_out, preferred_element_type=jnp.float32)
    attn_total, mamba_total = lax.psum((attn_square, mamba_square), "tp")
    attn_scale = jnp.sqrt(attn_total / (HQ * HD) + 1e-06)
    mamba_scale = jnp.sqrt(mamba_total / MI + 1e-06)
    partial_value = 0.5 * (attn_proj / attn_scale[:, None] + mamba_proj / mamba_scale[:, None])
    mixed = lax.psum_scatter(partial_value, "tp", scatter_dimension=1, tiled=True)
    column_width = model_width // tp_count
    residual = lax.dynamic_slice_in_dim(
        hidden_f, lax.axis_index("tp") * column_width, column_width, 1
    )
    layer_out = (residual + mixed).astype(jnp.bfloat16)
    return (layer_out, new_state)


def solution(mesh):
    return jax.shard_map(
        body,
        mesh=mesh,
        in_specs=(
            P("req", None),
            P(),
            P(None, "tp"),
            P(None, "tp"),
            P("tp", None),
            P("tp"),
            P(None, None, "tp"),
            P(None, "tp"),
            P("req", None, "tp"),
            P("tp", None),
            P(None, "tp"),
            P("tp"),
            P(None, "tp"),
            P("tp"),
            P("req", None, "tp"),
            P("tp"),
            P("tp", None),
            P("req", "tp", None, None),
            P(),
            P("req"),
            P("req"),
        ),
        out_specs=(P("req", "tp"), P("req", None, "tp")),
        check_vma=False,
    )
```

profile of v0, /device:TPU:1, one launch (start us, length us, event | category | flops | bytes accessed | tf_op | source)
XLA Modules:
  0.0 191.6 jit_solution(11031688939695422736)
XLA Ops:
  7.2 0.8 compare_and_fusion
  8.0 0.7 iota_compare_fusion
  8.7 0.9 multiply_reduce_fusion.3
  9.6 1.3 fusion.74
  10.9 0.8 dynamic-slice_convert_fusion
  11.6 0.1 multiply_cosine_fusion.1
  11.7 0.1 fusion.65
  11.9 1.7 fusion.69
  13.8 0.2 multiply_reduce_fusion.4
  14.0 53.3 %all_gather.3 = bf16[512,320]{1,0:T(8,128)(2,1)S(1)} all-gather(bf16[8,320]{1,0:T(8,128)(2,1)S(1)} %convert_element_type.89), channel_id=1, replica_groups=mesh['req'=64,'tp'=4] {'req'}, dimensions={0}, use_global_device_ids=true | all-gather | bytes 332800 | tf_op jit(solution)/shard_map/all_gather | solution.py:73
  67.4 0.8 gather_fusion
  68.2 0.6 gather_fusion.1
  68.8 0.1 gather.16
  69.1 3.6 %fusion.73 = (f32[34,5]{1,0:T(8,128)S(1)}, f32[34,5,512]{2,1,0:T(8,128)S(1)}) fusion(bf16[34,1,512,128]{3,2,1,0:T(8,128)(2,1)} %param.38, bf16[34,5,64]{2,1,0:T(8,128)(2,1)S(1)} %gather.16, pred[34]{0:T(512)(128)(4,1)S(1)} %get-tuple-element.14, pred[34,512]{1,0:T(8,128)(4,1)S(1)} %iota_compare_fusion.1), kind=kOutput, calls=%fused_computation.108 | convolution fusion | flops 11412950 | bytes 4844490 | tf_op jit(solution)/shard_map/shd,std->sht/dot_general | solution.py:83
  72.8 0.1 select_reduce_fusion
  72.9 0.1 copy.66
  73.1 0.6 gather_fusion.2
  73.8 0.3 convert_reduce_fusion
  74.0 0.2 fusion.48
  74.3 0.1 reshape.306
  74.4 0.8 copy.72
  75.2 6.0 %all-to-all-start.2 = ((f32[64,8,5]{1,2,0:T(8,128)}), f32[64,8,5]{1,2,0:T(8,128)S(1)}, u32[]{:S(2)}, u32[]{:S(2)}) async-start(f32[64,8,5]{1,2,0:T(8,128)} %copy.72), calls=%async_computation.2 | async-start | bytes 524288 | tf_op jit(solution)/shard_map/all_to_all | solution.py:113
  81.2 3.7 %fusion.20 = f32[34,5,64]{2,1,0:T(8,128)S(1)} fusion(bf16[34,1,512,128]{3,2,1,0:T(8,128)(2,1)} %param.38, f32[34,5]{1,0:T(8,128)S(1)} %subtract_exponential_fusion.1, f32[34,5,512]{2,1,0:T(8,128)S(1)} %get-tuple-element.29, f32[34,5]{1,0:T(8,128)S(1)} %get-tuple-element.28, pred[34,512]{1,0:T(8,128)(4,1)S(1)} %iota_compare_fusion.1), kind=kOutput, calls=%fused_computation.21 | convolution fusion | flops 11413120 | bytes 4866896 | tf_op jit(solution)/shard_map/sht,std->shd/dot_general | solution.py:92
  85.2 1.8 fusion.75
  87.0 0.1 fusion.77
  87.2 9.1 %psum.22 = f32[8,132]{1,0:T(8,128)S(1)} all-reduce(f32[8,132]{1,0:T(8,128)S(1)} %fusion.77), channel_id=1, replica_groups=mesh['req'=64,'tp'=4] {'tp'}, use_global_device_ids=true, to_apply=%region_10.11 | all-reduce | flops 1056 | bytes 8448 | tf_op jit(solution)/shard_map/psum | solution.py:147
  96.3 1.4 fusion.41
  97.7 0.2 fusion.76
  98.0 0.1 reshape.305
  98.1 0.8 copy.67
  98.9 12.1 %all-to-all-start.1 = ((f32[64,8,5]{1,2,0:T(8,128)}), f32[64,8,5]{1,2,0:T(8,128)S(1)}, u32[]{:S(2)}, u32[]{:S(2)}) async-start(f32[64,8,5]{1,2,0:T(8,128)} %copy.67), calls=%async_computation.1 | async-start | bytes 524288 | tf_op jit(solution)/shard_map/all_to_all | solution.py:120
  111.0 0.9 multiply_reduce_fusion.1
  111.9 11.1 %all-to-all-done.1 = f32[64,8,5]{1,2,0:T(8,128)S(1)} async-done(((f32[64,8,5]{1,2,0:T(8,128)}), f32[64,8,5]{1,2,0:T(8,128)S(1)}, u32[]{:S(2)}, u32[]{:S(2)}) %all-to-all-start.1) | async-done | bytes 10272 | tf_op jit(solution)/shard_map/all_to_all | solution.py:120
  123.0 6.0 %all-to-all-start = ((f32[64,8,320]{2,1,0:T(8,128)}), f32[64,8,320]{2,1,0:T(8,128)S(1)}, u32[]{:S(2)}, u32[]{:S(2)}) async-start(f32[64,8,320]{2,1,0:T(8,128)} %fusion.41), calls=%async_computation | async-start | bytes 1572864 | tf_op jit(solution)/shard_map/all_to_all | solution.py:106
  129.2 1.9 %multiply_reduce_fusion.5 = (f32[8]{0:T(128)S(1)}, f32[8,400]{1,0:T(8,128)S(1)}) fusion(bf16[2,1600,400]{1,2,0:T(8,128)(2,1)} %param.27, f32[1600]{0:T(1024)S(1)} %copy-done.7, f32[8]{0:T(128)S(1)} %add_rsqrt_fusion, bf16[8,1600]{1,0:T(8,128)(2,1)S(1)} %copy-done.3, f32[8,400]{1,0:T(8,128)S(1)} %get-tuple-element.4, ...), kind=kOutput, calls=%fused_computation.61 | convolution fusion | flops 10323192 | bytes 1396864 | tf_op jit(solution)/shard_map/dot_general | solution.py:141
  131.3 0.1 copy.69
  131.5 0.1 mul.364
  131.6 1.4 copy.70
  133.4 18.6 %all-to-all-done = f32[64,8,320]{2,1,0:T(8,128)S(1)} async-done(((f32[64,8,320]{2,1,0:T(8,128)}), f32[64,8,320]{2,1,0:T(8,128)S(1)}, u32[]{:S(2)}, u32[]{:S(2)}) %all-to-all-start) | async-done | bytes 655392 | tf_op jit(solution)/shard_map/all_to_all | solution.py:106
  152.0 1.3 multiply_reduce_fusion
  153.3 0.1 multiply_reduce_fusion.6
  153.4 6.1 %all-reduce = (f32[8]{0:T(128)S(1)}, f32[8]{0:T(128)S(1)}) all-reduce(f32[8]{0:T(128)S(1)} %get-tuple-element.6, f32[8]{0:T(128)S(1)} %get-tuple-element.36), channel_id=1, replica_groups=mesh['req'=64,'tp'=4] {'tp'}, use_global_device_ids=true, to_apply=%region_9.10 | all-reduce | flops 16 | bytes 128 | tf_op jit(solution)/shard_map/psum | solution.py:172
  159.6 0.3 convolution_divide_fusion.1
  159.9 0.3 fusion.7
  160.2 1.2 copy.74
  161.4 21.6 %reduce-scatter.4.cloned.1.call-done = f32[400,8]{1,0:T(8,128)} async-done(((f32[1600,8]{1,0:T(8,128)}), f32[400,8]{1,0:T(8,128)}) %reduce-scatter.4.cloned.1.call-update) | async-done | bytes 12816
  183.0 1.0 copy.75
  184.0 0.7 add_convert_fusion
  (66 shorter events, 1.8 us)
Async XLA Ops:
  7.2 152.7 %copy-start = (bf16[400,1600]{1,0:T(8,128)(2,1)S(1)}, bf16[400,1600]{1,0:T(8,128)(2,1)}, u32[]{:S(2)}) copy-start(bf16[400,1600]{1,0:T(8,128)(2,1)} %param.37) | copy-start | bytes 3840004
  7.2 60.2 %copy-start.1 = (s32[512]{0:T(512)S(1)}, s32[512]{0:T(512)}, u32[]{:S(2)}) copy-start(s32[512]{0:T(512)} %param.39) | copy-start | bytes 6148
  11.9 57.1 %copy-start.10 = (s32[34]{0:T(128)S(1)}, s32[34]{0:T(128)}, u32[]{:S(2)}) copy-start(s32[34]{0:T(128)} %param.40) | copy-start | bytes 412
  11.9 57.1 %copy-start.14 = (s32[34]{0:T(128)S(1)}, s32[34]{0:T(128)}, u32[]{:S(2)}) copy-start(s32[34]{0:T(128)} %param.41) | copy-start | bytes 412
  75.2 23.7 %all-to-all-start.2 = ((f32[64,8,5]{1,2,0:T(8,128)}), f32[64,8,5]{1,2,0:T(8,128)S(1)}, u32[]{:S(2)}, u32[]{:S(2)}) async-start(f32[64,8,5]{1,2,0:T(8,128)} %copy.72), calls=%async_computation.2 | async-start | bytes 524288 | tf_op jit(solution)/shard_map/all_to_all | solution.py:113
  81.2 3.9 %copy-start.9 = (f32[4,400]{1,0:T(4,128)S(1)}, f32[4,400]{1,0:T(4,128)}, u32[]{:S(2)}) copy-start(f32[4,400]{1,0:T(4,128)} %param.28) | copy-start | bytes 19204
  81.2 3.9 %copy-start.3 = (bf16[8,1600]{1,0:T(8,128)(2,1)S(1)}, bf16[8,1600]{1,0:T(8,128)(2,1)}, u32[]{:S(2)}) copy-start(bf16[8,1600]{1,0:T(8,128)(2,1)} %param.21) | copy-start | bytes 76804
  81.2 3.9 %copy-start.7 = (f32[1600]{0:T(1024)S(1)}, f32[1600]{0:T(1024)}, u32[]{:S(2)}) copy-start(f32[1600]{0:T(1024)} %param.22) | copy-start | bytes 19204
  85.0 2.1 %copy-start.5 = (bf16[400,132]{0,1:T(8,128)(2,1)S(1)}, bf16[400,132]{0,1:T(8,128)(2,1)}, u32[]{:S(2)}) copy-start(bf16[400,132]{0,1:T(8,128)(2,1)} %param.30) | copy-start | bytes 316804
  85.1 12.6 %copy-start.6 = (bf16[100,400]{0,1:T(8,128)(2,1)S(1)}, bf16[100,400]{0,1:T(8,128)(2,1)}, u32[]{:S(2)}) copy-start(bf16[100,400]{0,1:T(8,128)(2,1)} %param.31) | copy-start | bytes 240004
  85.1 12.6 %copy-start.11 = (f32[400]{0:T(512)S(1)}, f32[400]{0:T(512)}, u32[]{:S(2)}) copy-start(f32[400]{0:T(512)} %param.32) | copy-start | bytes 4804
  85.1 13.7 %copy-start.8 = (f32[16,400]{1,0:T(8,128)S(1)}, f32[16,400]{1,0:T(8,128)}, u32[]{:S(2)}) copy-start(f32[16,400]{1,0:T(8,128)} %param.33) | copy-start | bytes 76804
  87.0 24.0 %copy-start.4 = (f32[8,16,400]{2,1,0:T(8,128)S(1)}, f32[8,16,400]{2,1,0:T(8,128)}, u32[]{:S(2)}) copy-start(f32[8,16,400]{2,1,0:T(8,128)} %param.35) | copy-start | bytes 614404
  98.9 30.3 %copy-start.15 = (f32[400]{0:T(512)S(1)}, f32[400]{0:T(512)}, u32[]{:S(2)}) copy-start(f32[400]{0:T(512)} %param.34) | copy-start | bytes 4804
  98.9 24.1 %all-to-all-start.1 = ((f32[64,8,5]{1,2,0:T(8,128)}), f32[64,8,5]{1,2,0:T(8,128)S(1)}, u32[]{:S(2)}, u32[]{:S(2)}) async-start(f32[64,8,5]{1,2,0:T(8,128)} %copy.67), calls=%async_computation.1 | async-start | bytes 524288 | tf_op jit(solution)/shard_map/all_to_all | solution.py:120
  123.0 29.0 %all-to-all-start = ((f32[64,8,320]{2,1,0:T(8,128)}), f32[64,8,320]{2,1,0:T(8,128)S(1)}, u32[]{:S(2)}, u32[]{:S(2)}) async-start(f32[64,8,320]{2,1,0:T(8,128)} %fusion.41), calls=%async_computation | async-start | bytes 1572864 | tf_op jit(solution)/shard_map/all_to_all | solution.py:106
  129.0 54.0 %reduce-scatter.4.cloned.1.call-start = ((), (), s32[]{:S(2)}) async-start(), calls=%async_computation.4 | async-start | bytes 1024000
  133.0 26.6 %copy-start.2 = (bf16[320,1600]{1,0:T(8,128)(2,1)S(1)}, bf16[320,1600]{1,0:T(8,128)(2,1)}, u32[]{:S(2)}) copy-start(bf16[320,1600]{1,0:T(8,128)(2,1)} %param.25) | copy-start | bytes 3072004
  133.0 26.6 %copy-start.12 = (f32[320]{0:T(512)S(1)}, f32[320]{0:T(512)}, u32[]{:S(2)}) copy-start(f32[320]{0:T(512)} %param.26) | copy-start | bytes 3844
  133.4 26.4 %copy-start.13 = (f32[400]{0:T(512)S(1)}, f32[400]{0:T(512)}, u32[]{:S(2)}) copy-start(f32[400]{0:T(512)} %param.36) | copy-start | bytes 4804
Sparse Core Ops, SparseCore 0:
  161.5 21.4 reduce-scatter.3
where the time goes:
time: 193 us; the launch traced here: 192 us
  blocking collectives  68.6 us (36%)
  waiting for transfers between devices  51.3 us (27%)
  starting transfers between devices  24.1 us (12%)
  matrix products  16.5 us (9%)
  between operations  14.4 us (7%)
  local copies, waits for them, and re-layouts  8.94 us (5%)
  other arithmetic  7.63 us (4%)
    all_gather x1, blocking collectives, body(): lax.all_gather(query.reshape(row_count, head_count * head_dim), 'req', ax...  53.3 us
    unnamed x2, waiting for transfers between devices  21.6 us
    all_to_all x1, waiting for transfers between devices, body(): lax.all_to_all(part_out.reshape(holders, row_count, head_count * head_dim...  18.6 us
    all_to_all x1, starting transfers between devices, body(): lax.all_to_all(request_max.reshape(holders, row_count, head_count), 'req'...  12.1 us
    all_to_all x1, waiting for transfers between devices, body(): lax.all_to_all(request_max.reshape(holders, row_count, head_count), 'req'...  11.1 us
    psum x1, blocking collectives, body(): lax.psum(jnp.dot(activated, select_weight, preferred_element_type=jnp.flo...  9.12 us
    psum x1, blocking collectives, body(): attn_total, mamba_total = lax.psum((attn_square, mamba_square), 'tp')  6.15 us
    all_to_all x1, starting transfers between devices, body(): lax.all_to_all(part_out.reshape(holders, row_count, head_count * head_dim...  6.03 us
  transfers between devices with their start and end apart: 4, of which 3 were waited for; matrix products, arithmetic and copies ran while one was open for 7% of the time, Pallas kernels for 0%

commit v1 on v0

v1 whole, which is shorter than its diff:
```python
import math

import jax
import jax.numpy as jnp
import numpy as np
from jax import lax
from jax.experimental import pallas as pl
from jax.experimental.pallas import tpu as pltpu
from jax.sharding import PartitionSpec as P

F32 = jnp.float32
BF16 = jnp.bfloat16
NEG = -1e30
ROWS = 8
HEADS = 5
HD = 64
LANES = 128
SPAD = 40
TP_COLS = 400
TP_PAD = 512
NT = (((1,), (1,)), ((), ()))


def iota(shape, axis):
    return lax.broadcasted_iota(jnp.int32, shape, axis)


def dot(a, b):
    return jnp.dot(a, b, preferred_element_type=F32)


def dot_nt(a, b):
    return lax.dot_general(a, b, NT, preferred_element_type=F32)


def silu(v):
    return v * (1.0 / (1.0 + jnp.exp(-v)))


def softplus(v):
    return jnp.maximum(v, 0.0) + jnp.log1p(jnp.exp(-jnp.abs(v)))


LOCAL = (
    "len_s", "sr_s", "sb_s", "hidden", "gain", "freq", "wq", "wm", "mi", "cw", "cs", "sw", "st", "sb", "dl", "sg",
    "ss", "mg", "mo", "cache", "ag", "wo",
)


def kernel(n, tp_n, slots, *refs):
    hbm = dict(zip(LOCAL, refs[: len(LOCAL)]))
    out_layer, out_state = refs[len(LOCAL) : len(LOCAL) + 2]
    refs = refs[len(LOCAL) + 2 :]
    ref = dict(zip(LOCAL, refs[: len(LOCAL)]))
    (
        q_all, sel_buf, msg, inbox, m_send, m_recv, a_send, a_recv, q_slot, o_slot, state_v, layer_v, y_v,
        in_sem, out_sem, send_sem, recv_sem,
    ) = refs[len(LOCAL) :]
    me = lax.axis_index("req")
    tp = lax.axis_index("tp")

    copies = {}
    for k, name in enumerate(LOCAL):
        dst = ref[name].at[pl.ds(0, HEADS * HD)] if name == "wq" else ref[name]
        copies[name] = pltpu.make_async_copy(hbm[name], dst, in_sem.at[k])
        copies[name].start()

    barrier = pltpu.get_barrier_semaphore()

    def greet(i, carry):
        pl.semaphore_signal(barrier, inc=1, device_id={"req": lax.rem(me + i, n)})
        return carry

    lax.fori_loop(1, n, greet, 0)
    for i in range(1, tp_n):
        pl.semaphore_signal(barrier, inc=1, device_id={"tp": lax.rem(tp + i, tp_n)})

    def tp_start(src, dst, k):
        for i in range(1, tp_n):
            p = lax.rem(tp + i, tp_n)
            pltpu.make_async_remote_copy(
                src_ref=src(p), dst_ref=dst.at[tp], send_sem=send_sem.at[k], recv_sem=recv_sem.at[k],
                device_id={"tp": p},
            ).start()

    def wait_all(buf, k, count, which):
        view = buf.at[pl.ds(0, count)]
        copy = pltpu.make_async_remote_copy(
            src_ref=view, dst_ref=view, send_sem=send_sem.at[k], recv_sem=recv_sem.at[k], device_id={"tp": tp}
        )
        if which == "send":
            copy.wait_send()
        else:
            copy.wait_recv()

    lane8 = iota((ROWS, LANES), 1)
    low8 = lane8 < HD

    ref["wq"][pl.ds(HEADS * HD, 64), :] = jnp.zeros((64, ref["wq"].shape[1]), BF16)
    copies["hidden"].wait()
    copies["gain"].wait()
    hidden = ref["hidden"][...].astype(F32)
    width = hidden.shape[1]
    mean = jnp.sum(hidden * hidden, axis=1, keepdims=True) * (1.0 / width)
    normed = (hidden * lax.rsqrt(mean + 1e-06) * ref["gain"][...]).astype(BF16)

    for name in ("len_s", "sr_s", "sb_s", "freq"):
        copies[name].wait()
    position = jnp.zeros((ROWS, LANES), F32)
    row8 = iota((ROWS, LANES), 0)
    for r in range(ROWS):
        position = jnp.where(row8 == r, ref["len_s"][me * ROWS + r].astype(F32), position)
    angles = position * ref["freq"][...]
    cosine = jnp.cos(angles)
    sine = jnp.sin(angles)
    front = (lane8 & (HD - 1)) < HD // 2

    def rot(v):
        other = jnp.where(front, -pltpu.roll(v, LANES - HD // 2, 1), pltpu.roll(v, HD // 2, 1))
        return v * cosine + other * sine

    copies["wq"].wait()
    q_raw = dot_nt(normed, ref["wq"][...])
    query = [rot(q_raw[:, c * LANES : (c + 1) * LANES]).astype(BF16) for c in range(3)]
    for c in range(3):
        q_all[me, :, c * LANES : (c + 1) * LANES] = query[c]

    pl.semaphore_wait(barrier, n - 1 + tp_n - 1)

    def spread(i, carry):
        pltpu.make_async_remote_copy(
            src_ref=q_all.at[me], dst_ref=q_all.at[me], send_sem=send_sem.at[0], recv_sem=recv_sem.at[0],
            device_id={"req": lax.rem(me + i, n)},
        ).start()
        return carry

    lax.fori_loop(1, n, spread, 0)

    copies["mi"].wait()
    mamba_x = dot_nt(normed, ref["mi"][0]).astype(BF16)
    for name in ("cw", "cs", "sw"):
        copies[name].wait()
    taps = ref["cw"].shape[0]
    conv = ref["cw"][taps - 1 : taps, :] * mamba_x.astype(F32)
    for j in range(taps - 1):
        conv = conv + ref["cw"][j : j + 1, :] * ref["cs"][j].astype(F32)
    activated = silu(conv).astype(BF16)
    part = dot_nt(activated, ref["sw"][...])
    sel_buf[tp] = jnp.concatenate([part, jnp.zeros((ROWS, 2 * LANES - part.shape[1]), F32)], axis=1)
    tp_start(lambda p: sel_buf.at[tp], sel_buf, 1)

    gate = silu(dot_nt(normed, ref["mi"][1]))
    copies["wm"].wait()
    memory = dot(normed, ref["wm"][...])
    key_value = jnp.where(low8, rot(memory), memory).astype(BF16).astype(F32)
    swapped = pltpu.roll(key_value, HD, 1)
    key_both = jnp.where(low8, key_value, swapped)
    value_both = jnp.where(low8, swapped, key_value)

    own_score = []
    for h in range(HEADS):
        half = low8 if h % 2 == 0 else jnp.logical_not(low8)
        prod = jnp.where(half, query[h // 2].astype(F32) * key_both, 0.0)
        own_score.append(jnp.sum(prod, axis=1, keepdims=True) * HD**-0.5)

    lane40 = lax.rem(lane8, SPAD)
    lane40 = jnp.where(lane8 < 3 * SPAD, lane40, -1)
    sr_row = jnp.full((ROWS, LANES), -1, jnp.int32)
    sub_col = iota((SPAD, LANES), 0)
    sr_col = jnp.full((SPAD, LANES), -1, jnp.int32)
    for s in range(slots):
        v = ref["sr_s"][s]
        sr_row = jnp.where(lane40 == s, v, sr_row)
        sr_col = jnp.where(sub_col == s, v, sr_col)
    dest_row = lax.shift_right_arithmetic(sr_row, 3)
    rank_row = jnp.zeros((ROWS, LANES), jnp.int32)
    for s in range(slots):
        d = lax.shift_right_arithmetic(ref["sr_s"][s], 3)
        rank_row = rank_row + jnp.where((dest_row == d) & (lane40 > s), 1, 0)
    m_rows = n * 8
    mr = iota((m_rows, LANES), 0)
    mj = lax.shift_right_arithmetic(mr & 7, 1)
    cj = jnp.where(lane8 < SPAD, 0, jnp.where(lane8 < 2 * SPAD, 1, jnp.where(lane8 < 3 * SPAD, 2, -1)))
    pick = (
        (lax.shift_right_arithmetic(mr, 3) == dest_row[0:1, :])
        & ((mr & 1) == rank_row[0:1, :])
        & (mj == cj[0:1, :])
    )
    pick = jnp.where(pick, 1.0, 0.0).astype(BF16)
    own_pick = jnp.concatenate([sr_col] * (n * 8 // LANES), axis=1) if n * 8 >= LANES else sr_col[:, 0 : n * 8]
    own_pick = jnp.where(own_pick == iota((SPAD, n * 8), 1), 1.0, 0.0).astype(BF16)

    wait_all(sel_buf, 1, tp_n - 1, "recv")
    selection = sel_buf[0]
    for p in range(1, tp_n):
        selection = selection + sel_buf[p]
    dtr = ref["st"].shape[1]
    ns = ref["dl"].shape[0]
    for name in ("st", "sb", "dl", "sg", "ss", "mg", "mo"):
        copies[name].wait()
    step = softplus(dot_nt(selection[:, 0:dtr].astype(BF16), ref["st"][...]) + ref["sb"][...])
    maps = pltpu.roll(selection, selection.shape[1] - dtr, 1)[:, 0:LANES]
    maps = jnp.transpose(maps)
    active = activated.astype(F32)
    decay = jnp.exp(ref["dl"][...])
    drive = step * active
    for r in range(ROWS):
        new = (
            jnp.exp(-step[r : r + 1, :] * decay) * ref["ss"][r]
            + drive[r : r + 1, :] * maps[0:ns, r : r + 1]
        )
        state_v[r] = new
        y_v[r : r + 1, :] = jnp.sum(maps[ns : 2 * ns, r : r + 1] * new, axis=0, keepdims=True)
    state_out = pltpu.make_async_copy(state_v, out_state, out_sem.at[0])
    state_out.start()
    mamba_y = (y_v[...] + ref["sg"][...] * active) * gate

    def share(used, weight, square, send, recv, k):
        proj = dot(used, weight)
        extra = jnp.zeros((ROWS, 13 * LANES - proj.shape[1]), F32)
        proj = jnp.concatenate([proj, extra], axis=1)
        tail = iota((ROWS, TP_PAD), 1) >= TP_COLS
        for p in range(tp_n):
            moved = proj if p == 0 else pltpu.roll(proj, proj.shape[1] - p * TP_COLS, 1)
            send[p] = jnp.where(tail, square, moved[:, 0:TP_PAD])
        recv[tp] = send[tp]
        tp_start(lambda p: send.at[p], recv, k)

    def gathered(recv, k):
        wait_all(recv, k, tp_n - 1, "recv")
        total = recv[0]
        for p in range(1, tp_n):
            total = total + recv[p]
        return total

    mamba_square = jnp.sum(mamba_y * mamba_y, axis=1, keepdims=True)
    share((mamba_y * ref["mg"][...]).astype(BF16), ref["mo"][...], mamba_square, m_send, m_recv, 2)

    o_slot[...] = jnp.zeros_like(o_slot)
    q_slot[...] = jnp.zeros_like(q_slot)
    wait_all(q_all, 0, n - 1, "recv")
    q_sel = dot(own_pick, q_all[...].reshape(n * 8, 3 * LANES))
    low40 = iota((SPAD, LANES), 1) < HD
    for h in range(HEADS):
        col = q_sel[:, (h // 2) * LANES : (h // 2 + 1) * LANES]
        if h % 2 == 1:
            col = pltpu.roll(col, HD, 1)
        q_slot[h * SPAD : (h + 1) * SPAD, :] = jnp.where(low40, col, 0.0) * HD**-0.5
    copies["cache"].wait()
    block = ref["cache"].shape[1]
    time = iota((16, block), 1)
    first = iota((16, block), 0) < 8

    def live(s):
        owner = ref["sr_s"][s]
        used = owner >= 0
        return jnp.where(used, ref["len_s"][jnp.where(used, owner, 0)] - ref["sb_s"][s] * block, 0)

    def attend(p, carry):
        s0 = 2 * p
        s1 = s0 + 1
        pair = jnp.concatenate([ref["cache"][s0], ref["cache"][s1]], axis=1)
        q0 = q_slot[pl.ds(s0, 8, stride=SPAD), :]
        q1 = q_slot[pl.ds(s1, 8, stride=SPAD), :]
        zero = jnp.zeros_like(q0)
        lhs = jnp.concatenate(
            [jnp.concatenate([q0, zero], axis=1), jnp.concatenate([zero, q1], axis=1)], axis=0
        ).astype(BF16)
        scores = dot_nt(lhs, pair)
        ok = time < jnp.where(first, live(s0), live(s1))
        scores = jnp.where(ok, scores, NEG)
        top = jnp.max(scores, axis=1, keepdims=True)
        weights = jnp.where(ok, jnp.exp(scores - top), 0.0).astype(BF16)
        total = jnp.sum(weights.astype(F32), axis=1, keepdims=True)
        total = jnp.where(total > 0.0, total, 1.0)
        out = dot(weights, pair)
        lse = top + jnp.log(total)
        inv = 1.0 / total
        o_slot[pl.ds(s0, 8, stride=SPAD), :] = jnp.where(low8, lse[0:8], out[0:8, 0:LANES] * inv[0:8])
        o_slot[pl.ds(s1, 8, stride=SPAD), :] = jnp.where(low8, lse[8:16], out[8:16, LANES:] * inv[8:16])
        return carry

    lax.fori_loop(0, slots // 2, attend, 0)

    lane40v = iota((SPAD, LANES), 1)
    outs = [o_slot[h * SPAD : (h + 1) * SPAD, :] for h in range(HEADS)]
    turned = [pltpu.roll(o, HD, 1) for o in outs]
    tail = jnp.where(lane40v == 80, ((sr_col & 7) + 1).astype(F32), 0.0)
    for h in range(HEADS):
        rest = turned[h]
        for t in range(3):
            term = rest.astype(BF16).astype(F32)
            tail = jnp.where(lane40v == HD + 3 * h + t, term, tail)
            rest = rest - term
    table = jnp.concatenate(
        [
            jnp.where(low40, turned[0], outs[1]),
            jnp.where(low40, turned[2], outs[3]),
            jnp.where(low40, turned[4], tail),
            jnp.zeros((8, LANES), F32),
        ],
        axis=0,
    ).astype(BF16)
    msg[...] = dot(pick, table).reshape(n, 8, LANES).astype(BF16)
    inbox[me] = msg[me]

    def deliver(i, carry):
        d = lax.rem(me + i, n)
        pltpu.make_async_remote_copy(
            src_ref=msg.at[d], dst_ref=inbox.at[me], send_sem=send_sem.at[3], recv_sem=recv_sem.at[3],
            device_id={"req": d},
        ).start()
        return carry

    lax.fori_loop(1, n, deliver, 0)

    mamba = gathered(m_recv, 2)
    mamba_scale = jnp.sqrt(mamba[:, TP_COLS : TP_COLS + 1] * (1.0 / (TP_COLS * tp_n)) + 1e-06)
    wide = jnp.concatenate([hidden, jnp.zeros((ROWS, 13 * LANES - width), F32)], axis=1)
    residual = wide[:, 0:TP_PAD]
    for p in range(1, tp_n):
        residual = jnp.where(tp == p, pltpu.roll(wide, wide.shape[1] - p * TP_COLS, 1)[:, 0:TP_PAD], residual)
    base = residual + 0.5 * (mamba / mamba_scale)
    e_row = iota((16, LANES), 0)
    e_lane = iota((16, LANES), 1)
    e_start = HD + 3 * e_row
    spread_rows = ((e_row < HEADS) & (e_lane >= e_start) & (e_lane < e_start + 3)) | ((e_row == HEADS) & (e_lane == 80))
    spread_rows = jnp.where(spread_rows, 1.0, 0.0).astype(BF16)
    copies["ag"].wait()
    copies["wo"].wait()

    wait_all(inbox, 3, n - 1, "recv")
    box = inbox[...].reshape(n * 8, LANES)
    heads_row = dot_nt(spread_rows, box)
    col_j = lax.shift_right_arithmetic(iota((ROWS, n * 8), 1) & 7, 1)
    r_id = (iota((ROWS, n * 8), 0) + 1).astype(F32)
    shifted = [pltpu.roll(heads_row, n * 8 - (4 - 2 * j), 1) if j < 2 else heads_row for j in range(3)]
    high, low, den, own_w = [], [], [], []
    for h in range(HEADS):
        j = h // 2
        lse = jnp.broadcast_to(shifted[j][h : h + 1, :], (ROWS, n * 8))
        rid = jnp.broadcast_to(shifted[j][HEADS : HEADS + 1, :], (ROWS, n * 8))
        mine = (rid == r_id) & (col_j == j)
        top = jnp.maximum(jnp.max(jnp.where(mine, lse, NEG), axis=1, keepdims=True), own_score[h])
        w = jnp.where(mine, jnp.exp(lse - top), 0.0)
        own = jnp.exp(own_score[h] - top)
        den.append(jnp.sum(w, axis=1, keepdims=True) + own)
        own_w.append(own)
        w_high = w.astype(BF16).astype(F32)
        high.append(w_high)
        low.append(w - w_high)
    merged = dot(jnp.concatenate(high + low, axis=0).astype(BF16), box)
    numer = [
        merged[h * 8 : h * 8 + 8] + merged[(HEADS + h) * 8 : (HEADS + h) * 8 + 8] + own_w[h] * value_both
        for h in range(HEADS)
    ]
    normal = [numer[h] / den[h] for h in range(HEADS)]
    attention = jnp.concatenate(
        [
            jnp.where(low8, normal[0], normal[1]),
            jnp.where(low8, normal[2], normal[3]),
            jnp.where(low8, normal[4], 0.0),
        ],
        axis=1,
    )[:, 0 : HEADS * HD]
    attn_square = jnp.sum(attention * attention, axis=1, keepdims=True)
    share((attention * ref["ag"][...]).astype(BF16), ref["wo"][...], attn_square, a_send, a_recv, 4)
    attn = gathered(a_recv, 4)
    attn_scale = jnp.sqrt(attn[:, TP_COLS : TP_COLS + 1] * (1.0 / (HEADS * HD * tp_n)) + 1e-06)
    final = base + 0.5 * (attn / attn_scale)
    layer_v[...] = final[:, 0:TP_COLS].astype(BF16)
    layer_out = pltpu.make_async_copy(layer_v, out_layer, out_sem.at[1])
    layer_out.start()
    wait_all(q_all, 0, n - 1, "send")
    wait_all(sel_buf, 1, tp_n - 1, "send")
    wait_all(m_send, 2, tp_n - 1, "send")
    wait_all(msg, 3, n - 1, "send")
    wait_all(a_send, 4, tp_n - 1, "send")
    state_out.wait()
    layer_out.wait()


def body(
    hidden_in, norm_gain, query_weight, memory_weight, attention_out, attention_gain, mamba_input, conv_weight,
    conv_state, select_weight, step_weight, step_bias, decay_log, skip_gain, scan_state, mamba_gain, mamba_out,
    cache_blocks, lengths, slot_request, slot_block,
):
    n = lax.axis_size("req")
    tp_n = lax.axis_size("tp")
    slots, _, block, kv = cache_blocks.shape
    rate = 10000.0 ** (-(np.arange(LANES) % (HD // 2)) * (2.0 / HD))
    freq = jnp.asarray(np.broadcast_to(rate[None, :], (ROWS, LANES)), F32)
    row = lambda v: v.reshape(1, -1)
    operand = {
        "len_s": lengths,
        "sr_s": slot_request,
        "sb_s": slot_block,
        "hidden": hidden_in,
        "gain": row(norm_gain),
        "freq": freq,
        "wq": query_weight.T,
        "wm": memory_weight,
        "mi": jnp.transpose(mamba_input, (0, 2, 1)),
        "cw": conv_weight,
        "cs": jnp.transpose(conv_state, (1, 0, 2)),
        "sw": select_weight.T,
        "st": step_weight.T,
        "sb": row(step_bias),
        "dl": decay_log,
        "sg": row(skip_gain),
        "ss": scan_state,
        "mg": row(mamba_gain),
        "mo": mamba_out,
        "cache": cache_blocks.reshape(slots, block, kv),
        "ag": row(attention_gain),
        "wo": attention_out,
    }
    operand = [operand[name] for name in LOCAL]
    scratch = []
    for name, v in zip(LOCAL, operand):
        space = pltpu.SMEM if name in ("len_s", "sr_s", "sb_s") else pltpu.VMEM
        shape = (v.shape[0] + 64, v.shape[1]) if name == "wq" else v.shape
        scratch.append(space(shape, v.dtype))
    scratch += [
        pltpu.VMEM((n, ROWS, 3 * LANES), BF16),
        pltpu.VMEM((tp_n, ROWS, 2 * LANES), F32),
        pltpu.VMEM((n, 8, LANES), BF16),
        pltpu.VMEM((n, 8, LANES), BF16),
        pltpu.VMEM((tp_n, ROWS, TP_PAD), F32),
        pltpu.VMEM((tp_n, ROWS, TP_PAD), F32),
        pltpu.VMEM((tp_n, ROWS, TP_PAD), F32),
        pltpu.VMEM((tp_n, ROWS, TP_PAD), F32),
        pltpu.VMEM((8 * SPAD, LANES), F32),
        pltpu.VMEM((8 * SPAD, LANES), F32),
        pltpu.VMEM(scan_state.shape, F32),
        pltpu.VMEM((ROWS, TP_COLS), BF16),
        pltpu.VMEM((ROWS, TP_COLS), F32),
        pltpu.SemaphoreType.DMA((len(LOCAL),)),
        pltpu.SemaphoreType.DMA((2,)),
        pltpu.SemaphoreType.DMA((5,)),
        pltpu.SemaphoreType.DMA((5,)),
    ]

    def step(*refs):
        kernel(n, tp_n, slots, *refs)

    return pl.pallas_call(
        step,
        out_shape=(
            jax.ShapeDtypeStruct((ROWS, TP_COLS), BF16),
            jax.ShapeDtypeStruct(scan_state.shape, F32),
        ),
        in_specs=[pl.BlockSpec(memory_space=pl.ANY)] * len(operand),
        out_specs=(pl.BlockSpec(memory_space=pl.ANY),) * 2,
        scratch_shapes=scratch,
        compiler_params=pltpu.CompilerParams(collective_id=0, has_side_effects=True),
        name="decode_layer",
    )(*operand)


def solution(mesh):
    return jax.shard_map(
        body,
        mesh=mesh,
        in_specs=(
            P("req", None),
            P(),
            P(None, "tp"),
            P(None, "tp"),
            P("tp", None),
            P("tp"),
            P(None, None, "tp"),
            P(None, "tp"),
            P("req", None, "tp"),
            P("tp", None),
            P(None, "tp"),
            P("tp"),
            P(None, "tp"),
            P("tp"),
            P("req", None, "tp"),
            P("tp"),
            P("tp", None),
            P("req", "tp", None, None),
            P(),
            P("req"),
            P("req"),
        ),
        out_specs=(P("req", "tp"), P("req", None, "tp")),
        check_vma=False,
    )
```

time: 193 us -> 49.6 us (0.26)
  blocking collectives: 68.6 us -> 0 us
  waiting for transfers between devices: 51.3 us -> 0 us
  Pallas kernels: 0 us -> 43.2 us
  starting transfers between devices: 24.1 us -> 0 us
  matrix products: 16.5 us -> 0 us
  between operations: 14.4 us -> 0.64 us
  other arithmetic: 7.63 us -> 0 us
  local copies, waits for them, and re-layouts: 8.94 us -> 5.51 us
    all_gather x1 -> x0, blocking collectives: 53.3 us -> none  [body(): lax.all_gather(query.reshape(row_count, head_count * head_dim), 'req', ax...]
    pallas_call x0 -> x1, Pallas kernels: none -> 43.2 us  [body(): pl.pallas_call(step, out_shape=(jax.ShapeDtypeStruct((ROWS, TP_COLS), BF1...]
    all_to_all x3 -> x0, waiting for transfers between devices: 29.7 us -> none  [the longest x1 18.6 us: body(): lax.all_to_all(part_out.reshape(holders, row_count, head_count * head_dim...]
    all_to_all x3 -> x0, starting transfers between devices: 24.1 us -> none  [the longest x1 12.1 us: body(): lax.all_to_all(request_max.reshape(holders, row_count, head_count), 'req'...]
    unnamed x2 -> x0, waiting for transfers between devices: 21.6 us -> none
    dot_general x12 -> x0, matrix products: 16.5 us -> none  [the longest x1 3.73 us: body(): jnp.einsum('sht,std->shd', weights, values, preferred_element_type=jnp.fl...]
    psum x2 -> x0, blocking collectives: 15.3 us -> none  [the longest x1 9.12 us: body(): lax.psum(jnp.dot(activated, select_weight, preferred_element_type=jnp.flo...]
    reduce_sum x7 -> x0, other arithmetic: 3.67 us -> none  [the longest x1 1.28 us: body(): jnp.sum(got_out.reshape(holders, row_count, head_count, head_dim) * sourc...]
  transfers between devices with their start and end apart: 4 -> 0, of which waited for: 3 -> 0; matrix products, arithmetic and copies ran while one was open for 7% -> 0% of each run, Pallas kernels for 0% -> 0%
where the time goes in v1:
time: 49.6 us; the launch traced here: 49.4 us
  Pallas kernels  43.2 us (87%)
  local copies, waits for them, and re-layouts  5.51 us (11%)
  between operations  0.64 us (1%)
    pallas_call x1, Pallas kernels, body(): pl.pallas_call(step, out_shape=(jax.ShapeDtypeStruct((ROWS, TP_COLS), BF1...  43.2 us
    unnamed x2, local copies, waits for them, and re-layouts  2.97 us
    reshape x2, local copies, waits for them, and re-layouts, body(): row = lambda v: v.reshape(1, -1)  2.54 us

profile of v1, /device:TPU:1, one launch (start us, length us, event | category | flops | bytes accessed | tf_op | source)
XLA Modules:
  0.0 49.4 jit_solution(8509873514447309372)
XLA Ops:
  0.6 1.2 %reshape.27.refs_20_ = f32[1,320]{1,0:T(1,128)} reshape(f32[320]{0:T(512)} %param.27) | data formatting | bytes 2560 | tf_op jit(solution)/shard_map/reshape | solution.py:393
  1.9 1.3 %reshape.22.refs_4_ = f32[1,1600]{1,0:T(1,128)} reshape(f32[1600]{0:T(1024)} %param.23) | data formatting | bytes 12800 | tf_op jit(solution)/shard_map/reshape | solution.py:393
  3.2 43.2 %decode_layer.1 = (bf16[8,400]{1,0:T(8,128)(2,1)}, f32[8,16,400]{2,1,0:T(8,128)}) custom-call(s32[512]{0:T(512)} %refs_0_.1, s32[34]{0:T(128)} %refs_1_.1, s32[34]{0:T(128)} %refs_2_.1, bf16[8,1600]{1,0:T(8,128)(2,1)} %refs_3_.1, f32[1,1600]{1,0:T(1,128)} %reshape.22.refs_4_, f32[8,128]{1,0:T(8,128)} %constant.2.clone.refs_5_, bf16[320,1600]{1,0:T(8,128)(2,1)} %bitcast.11, ...), custom_call_target="tpu_custom_call" | custom-call | tf_op jit(solution)/shard_map/decode_layer/pallas_call | solution.py:447
  46.4 1.3 %copy.26 = bf16[8,400]{1,0:T(8,128)(2,1)} copy(bf16[8,400]{1,0:T(8,128)(2,1)} %get-tuple-element.4) | data formatting | bytes 12800
  47.7 1.7 %copy.27 = f32[8,16,400]{2,1,0:T(8,128)} copy(f32[8,16,400]{2,1,0:T(8,128)} %get-tuple-element.5) | data formatting | bytes 409600

commit v2 on v1

--- a/solution.py
+++ b/solution.py
@@ -21,6 +21,10 @@
 NT = (((1,), (1,)), ((), ()))
 
 
+def depth_of(n):
+    return 8 if n >= 32 else n // 4
+
+
 def iota(shape, axis):
     return lax.broadcasted_iota(jnp.int32, shape, axis)
 
@@ -53,11 +57,24 @@
     refs = refs[len(LOCAL) + 2 :]
     ref = dict(zip(LOCAL, refs[: len(LOCAL)]))
     (
-        q_all, sel_buf, msg, inbox, m_send, m_recv, a_send, a_recv, q_slot, o_slot, state_v, layer_v, y_v,
-        in_sem, out_sem, send_sem, recv_sem,
+        q_all, sel_buf, msg, inbox, m_send, m_recv, a_send, a_recv, q_slot, o_slot, y_v,
+        in_sem, send_sem, recv_sem, z_sem,
     ) = refs[len(LOCAL) :]
     me = lax.axis_index("req")
     tp = lax.axis_index("tp")
+
+    z_n = depth_of(n)
+    plane_n = n // z_n
+    core = lax.rem(me, 2)
+    z = lax.rem(me // 2, z_n)
+    place = me // (2 * z_n) * 2 + core
+
+    def at(place, z):
+        return place // 2 * (2 * z_n) + z * 2 + lax.rem(place, 2)
+
+    z_order = sorted(range(1, z_n), key=lambda i: (min(i, z_n - i), i))
+    column = {i: at(place, lax.rem(z + i, z_n)) for i in z_order}
+    plane = [at(lax.rem(place + j, plane_n), z) for j in range(1, plane_n)]
 
     copies = {}
     for k, name in enumerate(LOCAL):
@@ -66,14 +83,13 @@
         copies[name].start()
 
     barrier = pltpu.get_barrier_semaphore()
-
-    def greet(i, carry):
-        pl.semaphore_signal(barrier, inc=1, device_id={"req": lax.rem(me + i, n)})
-        return carry
-
-    lax.fori_loop(1, n, greet, 0)
+    for i in reversed(z_order):
+        pl.semaphore_signal(barrier, inc=1, device_id={"req": column[i]})
+    for d in plane:
+        pl.semaphore_signal(barrier, inc=1, device_id={"req": d})
     for i in range(1, tp_n):
         pl.semaphore_signal(barrier, inc=1, device_id={"tp": lax.rem(tp + i, tp_n)})
+    inbox[...] = jnp.zeros_like(inbox)
 
     def tp_start(src, dst, k):
         for i in range(1, tp_n):
@@ -84,7 +100,7 @@
             ).start()
 
     def wait_all(buf, k, count, which):
-        view = buf.at[pl.ds(0, count)]
+        view = buf.at[pl.ds(0, count), pl.ds(0, 6)] if k == 3 else buf.at[pl.ds(0, count)]
         copy = pltpu.make_async_remote_copy(
             src_ref=view, dst_ref=view, send_sem=send_sem.at[k], recv_sem=recv_sem.at[k], device_id={"tp": tp}
         )
@@ -102,7 +118,7 @@
     hidden = ref["hidden"][...].astype(F32)
     width = hidden.shape[1]
     mean = jnp.sum(hidden * hidden, axis=1, keepdims=True) * (1.0 / width)
-    normed = (hidden * lax.rsqrt(mean + 1e-06) * ref["gain"][...]).astype(BF16)
+    normed = (hidden * lax.rsqrt(mean + 1e-06) * ref["gain"][...].reshape(1, width)).astype(BF16)
 
     for name in ("len_s", "sr_s", "sb_s", "freq"):
         copies[name].wait()
@@ -125,16 +141,31 @@
     for c in range(3):
         q_all[me, :, c * LANES : (c + 1) * LANES] = query[c]
 
-    pl.semaphore_wait(barrier, n - 1 + tp_n - 1)
-
-    def spread(i, carry):
-        pltpu.make_async_remote_copy(
-            src_ref=q_all.at[me], dst_ref=q_all.at[me], send_sem=send_sem.at[0], recv_sem=recv_sem.at[0],
-            device_id={"req": lax.rem(me + i, n)},
-        ).start()
-        return carry
-
-    lax.fori_loop(1, n, spread, 0)
+    pl.semaphore_wait(barrier, len(z_order) + len(plane) + tp_n - 1)
+
+    def z_copy(i, source, target):
+        return pltpu.make_async_remote_copy(
+            src_ref=q_all.at[source], dst_ref=q_all.at[source], send_sem=send_sem.at[0], recv_sem=z_sem.at[i - 1],
+            device_id={"req": target},
+        )
+
+    def pass_on(source):
+        for d in plane:
+            pltpu.make_async_remote_copy(
+                src_ref=q_all.at[source], dst_ref=q_all.at[source], send_sem=send_sem.at[0], recv_sem=recv_sem.at[0],
+                device_id={"req": d},
+            ).start()
+
+    def pass_on_from(distance):
+        for i in z_order:
+            if min(i, z_n - i) == distance:
+                source = at(place, lax.rem(z + z_n - i, z_n))
+                z_copy(i, source, source).wait_recv()
+                pass_on(source)
+
+    for i in reversed(z_order):
+        z_copy(i, me, column[i]).start()
+    pass_on(me)
 
     copies["mi"].wait()
     mamba_x = dot_nt(normed, ref["mi"][0]).astype(BF16)
@@ -149,7 +180,9 @@
     sel_buf[tp] = jnp.concatenate([part, jnp.zeros((ROWS, 2 * LANES - part.shape[1]), F32)], axis=1)
     tp_start(lambda p: sel_buf.at[tp], sel_buf, 1)
 
+    pass_on_from(1)
     gate = silu(dot_nt(normed, ref["mi"][1]))
+    pass_on_from(2)
     copies["wm"].wait()
     memory = dot(normed, ref["wm"][...])
     key_value = jnp.where(low8, rot(memory), memory).astype(BF16).astype(F32)
@@ -163,6 +196,7 @@
         prod = jnp.where(half, query[h // 2].astype(F32) * key_both, 0.0)
         own_score.append(jnp.sum(prod, axis=1, keepdims=True) * HD**-0.5)
 
+    pass_on_from(3)
     lane40 = lax.rem(lane8, SPAD)
     lane40 = jnp.where(lane8 < 3 * SPAD, lane40, -1)
     sr_row = jnp.full((ROWS, LANES), -1, jnp.int32)
@@ -190,6 +224,8 @@
     own_pick = jnp.concatenate([sr_col] * (n * 8 // LANES), axis=1) if n * 8 >= LANES else sr_col[:, 0 : n * 8]
     own_pick = jnp.where(own_pick == iota((SPAD, n * 8), 1), 1.0, 0.0).astype(BF16)
 
+    for distance in range(4, z_n // 2 + 1):
+        pass_on_from(distance)
     wait_all(sel_buf, 1, tp_n - 1, "recv")
     selection = sel_buf[0]
     for p in range(1, tp_n):
@@ -209,10 +245,8 @@
             jnp.exp(-step[r : r + 1, :] * decay) * ref["ss"][r]
             + drive[r : r + 1, :] * maps[0:ns, r : r + 1]
         )
-        state_v[r] = new
+        out_state[r] = new
         y_v[r : r + 1, :] = jnp.sum(maps[ns : 2 * ns, r : r + 1] * new, axis=0, keepdims=True)
-    state_out = pltpu.make_async_copy(state_v, out_state, out_sem.at[0])
-    state_out.start()
     mamba_y = (y_v[...] + ref["sg"][...] * active) * gate
 
     def share(used, weight, square, send, recv, k):
@@ -238,7 +272,7 @@
 
     o_slot[...] = jnp.zeros_like(o_slot)
     q_slot[...] = jnp.zeros_like(q_slot)
-    wait_all(q_all, 0, n - 1, "recv")
+    wait_all(q_all, 0, n - z_n, "recv")
     q_sel = dot(own_pick, q_all[...].reshape(n * 8, 3 * LANES))
     low40 = iota((SPAD, LANES), 1) < HD
     for h in range(HEADS):
@@ -280,7 +314,7 @@
         o_slot[pl.ds(s1, 8, stride=SPAD), :] = jnp.where(low8, lse[8:16], out[8:16, LANES:] * inv[8:16])
         return carry
 
-    lax.fori_loop(0, slots // 2, attend, 0)
+    lax.fori_loop(0, slots // 2, attend, 0, unroll=True)
 
     lane40v = iota((SPAD, LANES), 1)
     outs = [o_slot[h * SPAD : (h + 1) * SPAD, :] for h in range(HEADS)]
@@ -307,12 +341,12 @@
     def deliver(i, carry):
         d = lax.rem(me + i, n)
         pltpu.make_async_remote_copy(
-            src_ref=msg.at[d], dst_ref=inbox.at[me], send_sem=send_sem.at[3], recv_sem=recv_sem.at[3],
+            src_ref=msg.at[d, pl.ds(0, 6)], dst_ref=inbox.at[me, pl.ds(0, 6)], send_sem=send_sem.at[3], recv_sem=recv_sem.at[3],
             device_id={"req": d},
         ).start()
         return carry
 
-    lax.fori_loop(1, n, deliver, 0)
+    lax.fori_loop(1, n, deliver, 0, unroll=7)
 
     mamba = gathered(m_recv, 2)
     mamba_scale = jnp.sqrt(mamba[:, TP_COLS : TP_COLS + 1] * (1.0 / (TP_COLS * tp_n)) + 1e-06)
@@ -364,20 +398,25 @@
         axis=1,
     )[:, 0 : HEADS * HD]
     attn_square = jnp.sum(attention * attention, axis=1, keepdims=True)
-    share((attention * ref["ag"][...]).astype(BF16), ref["wo"][...], attn_square, a_send, a_recv, 4)
+    share((attention * ref["ag"][...].reshape(1, HEADS * HD)).astype(BF16), ref["wo"][...], attn_square, a_send, a_recv, 4)
     attn = gathered(a_recv, 4)
     attn_scale = jnp.sqrt(attn[:, TP_COLS : TP_COLS + 1] * (1.0 / (HEADS * HD * tp_n)) + 1e-06)
     final = base + 0.5 * (attn / attn_scale)
-    layer_v[...] = final[:, 0:TP_COLS].astype(BF16)
-    layer_out = pltpu.make_async_copy(layer_v, out_layer, out_sem.at[1])
-    layer_out.start()
+    out_layer[...] = final[:, 0:TP_COLS].astype(BF16)
     wait_all(q_all, 0, n - 1, "send")
     wait_all(sel_buf, 1, tp_n - 1, "send")
     wait_all(m_send, 2, tp_n - 1, "send")
     wait_all(msg, 3, n - 1, "send")
     wait_all(a_send, 4, tp_n - 1, "send")
-    state_out.wait()
-    layer_out.wait()
+
+
+def write_out(layer, state, layer_out, state_out, sem):
+    first = pltpu.make_async_copy(state, state_out, sem.at[0])
+    second = pltpu.make_async_copy(layer, layer_out, sem.at[1])
+    first.start()
+    second.start()
+    first.wait()
+    second.wait()
 
 
 def body(
@@ -396,7 +435,7 @@
         "sr_s": slot_request,
         "sb_s": slot_block,
         "hidden": hidden_in,
-        "gain": row(norm_gain),
+        "gain": norm_gain,
         "freq": freq,
         "wq": query_weight.T,
         "wm": memory_weight,
@@ -412,10 +451,10 @@
         "mg": row(mamba_gain),
         "mo": mamba_out,
         "cache": cache_blocks.reshape(slots, block, kv),
-        "ag": row(attention_gain),
+        "ag": attention_gain,
         "wo": attention_out,
     }
-    operand = [operand[name] for name in LOCAL]
+    operand = [pltpu.with_memory_space_constraint(operand[name], pltpu.HBM) for name in LOCAL]
     scratch = []
     for name, v in zip(LOCAL, operand):
         space = pltpu.SMEM if name in ("len_s", "sr_s", "sb_s") else pltpu.VMEM
@@ -432,30 +471,38 @@
         pltpu.VMEM((tp_n, ROWS, TP_PAD), F32),
         pltpu.VMEM((8 * SPAD, LANES), F32),
         pltpu.VMEM((8 * SPAD, LANES), F32),
-        pltpu.VMEM(scan_state.shape, F32),
-        pltpu.VMEM((ROWS, TP_COLS), BF16),
         pltpu.VMEM((ROWS, TP_COLS), F32),
         pltpu.SemaphoreType.DMA((len(LOCAL),)),
-        pltpu.SemaphoreType.DMA((2,)),
         pltpu.SemaphoreType.DMA((5,)),
         pltpu.SemaphoreType.DMA((5,)),
+        pltpu.SemaphoreType.DMA((max(1, depth_of(n) - 1),)),
     ]
 
     def step(*refs):
         kernel(n, tp_n, slots, *refs)
 
-    return pl.pallas_call(
+    layer, state = pl.pallas_call(
         step,
         out_shape=(
             jax.ShapeDtypeStruct((ROWS, TP_COLS), BF16),
             jax.ShapeDtypeStruct(scan_state.shape, F32),
         ),
-        in_specs=[pl.BlockSpec(memory_space=pl.ANY)] * len(operand),
-        out_specs=(pl.BlockSpec(memory_space=pl.ANY),) * 2,
+        in_specs=[pl.BlockSpec(memory_space=pltpu.HBM)] * len(operand),
+        out_specs=(pl.BlockSpec(memory_space=pltpu.VMEM),) * 2,
         scratch_shapes=scratch,
-        compiler_params=pltpu.CompilerParams(collective_id=0, has_side_effects=True),
+        compiler_params=pltpu.CompilerParams(collective_id=0, has_side_effects=True, vmem_limit_bytes=24 << 20),
         name="decode_layer",
     )(*operand)
+    results = (jax.ShapeDtypeStruct(layer.shape, BF16), jax.ShapeDtypeStruct(state.shape, F32))
+    return pl.pallas_call(
+        write_out,
+        out_shape=results,
+        in_specs=[pl.BlockSpec(memory_space=pltpu.VMEM)] * 2,
+        out_specs=(pl.BlockSpec(memory_space=pl.ANY),) * 2,
+        scratch_shapes=[pltpu.SemaphoreType.DMA((2,))],
+        compiler_params=pltpu.CompilerParams(vmem_limit_bytes=1 << 20),
+        name="write_out",
+    )(layer, state)
 
 
 def solution(mesh):

time: 49.6 us -> 36.7 us (0.74)
  Pallas kernels: 43.2 us -> 36 us
  local copies, waits for them, and re-layouts: 5.51 us -> 0 us
    pallas_call x1, Pallas kernels: 43.2 us -> 35.3 us  [body(): pl.pallas_call(step, out_shape=(jax.ShapeDtypeStruct((ROWS, TP_COLS), BF1...]
    unnamed x2 -> x0, local copies, waits for them, and re-layouts: 2.97 us -> none
    reshape x2 -> x0, local copies, waits for them, and re-layouts: 2.54 us -> none  [body(): row = lambda v: v.reshape(1, -1)]
    pallas_call x0 -> x1, Pallas kernels: none -> 0.72 us  [body(): pl.pallas_call(write_out, out_shape=results, in_specs=[pl.BlockSpec(memor...]
where the time goes in v2:
time: 36.7 us
  Pallas kernels  36 us (98%)
  between operations  0.65 us (2%)
    pallas_call x1, Pallas kernels, body(): pl.pallas_call(step, out_shape=(jax.ShapeDtypeStruct((ROWS, TP_COLS), BF1...  35.3 us

profile of v2, /device:TPU:1, one launch (start us, length us, event | category | flops | bytes accessed | tf_op | source)
XLA Modules:
  0.0 36.7 jit_solution(12163534901654829461)
XLA Ops:
  0.6 35.3 %decode_layer.1 = (bf16[8,400]{1,0:T(8,128)(2,1)S(1)}, f32[8,16,400]{2,1,0:T(8,128)S(1)}) custom-call(s32[512]{0:T(512)} %refs_0_.1, s32[34]{0:T(128)} %refs_1_.1, s32[34]{0:T(128)} %refs_2_.1, bf16[8,1600]{1,0:T(8,128)(2,1)} %refs_3_.1, f32[1600]{0:T(1024)} %refs_4_.1, f32[8,128]{1,0:T(8,128)} %constant.2.clone.refs_5_, bf16[320,1600]{1,0:T(8,128)(2,1)} %bitcast.11, ...), custom_call_target="tpu_custom_call" | custom-call | tf_op jit(solution)/shard_map/decode_layer/pallas_call | solution.py:484
  35.9 0.7 %write_out.1 = (bf16[8,400]{1,0:T(8,128)(2,1)}, f32[8,16,400]{2,1,0:T(8,128)}) custom-call(bf16[8,400]{1,0:T(8,128)(2,1)S(1)} %get-tuple-element.4.layer, f32[8,16,400]{2,1,0:T(8,128)S(1)} %get-tuple-element.5.state), custom_call_target="tpu_custom_call" | custom-call | tf_op jit(solution)/shard_map/write_out/pallas_call | solution.py:497

commit v3 on v2

--- a/solution.py
+++ b/solution.py
@@ -58,10 +58,17 @@
     ref = dict(zip(LOCAL, refs[: len(LOCAL)]))
     (
         q_all, sel_buf, msg, inbox, m_send, m_recv, a_send, a_recv, q_slot, o_slot, y_v,
+        keys, values, scores_v, weights_v, stat_v,
         in_sem, send_sem, recv_sem, z_sem,
     ) = refs[len(LOCAL) :]
     me = lax.axis_index("req")
     tp = lax.axis_index("tp")
+
+    copies = {}
+    for k, name in enumerate(LOCAL):
+        dst = ref[name].at[pl.ds(0, HEADS * HD)] if name == "wq" else ref[name]
+        copies[name] = pltpu.make_async_copy(hbm[name], dst, in_sem.at[k])
+        copies[name].start()
 
     z_n = depth_of(n)
     plane_n = n // z_n
@@ -75,12 +82,6 @@
     z_order = sorted(range(1, z_n), key=lambda i: (min(i, z_n - i), i))
     column = {i: at(place, lax.rem(z + i, z_n)) for i in z_order}
     plane = [at(lax.rem(place + j, plane_n), z) for j in range(1, plane_n)]
-
-    copies = {}
-    for k, name in enumerate(LOCAL):
-        dst = ref[name].at[pl.ds(0, HEADS * HD)] if name == "wq" else ref[name]
-        copies[name] = pltpu.make_async_copy(hbm[name], dst, in_sem.at[k])
-        copies[name].start()
 
     barrier = pltpu.get_barrier_semaphore()
     for i in reversed(z_order):
@@ -90,6 +91,10 @@
     for i in range(1, tp_n):
         pl.semaphore_signal(barrier, inc=1, device_id={"tp": lax.rem(tp + i, tp_n)})
     inbox[...] = jnp.zeros_like(inbox)
+    o_slot[...] = jnp.zeros_like(o_slot)
+    q_slot[...] = jnp.zeros_like(q_slot)
+    block = ref["cache"].shape[1]
+    quad_n = (slots + 3) // 4
 
     def tp_start(src, dst, k):
         for i in range(1, tp_n):
@@ -180,23 +185,27 @@
     sel_buf[tp] = jnp.concatenate([part, jnp.zeros((ROWS, 2 * LANES - part.shape[1]), F32)], axis=1)
     tp_start(lambda p: sel_buf.at[tp], sel_buf, 1)
 
+    def pack(quads):
+        for g in quads:
+            for c in range(2):
+                s0 = 4 * g + 2 * c
+                lanes = slice(c * LANES, (c + 1) * LANES)
+                if s0 < slots:
+                    one, two = ref["cache"][s0], ref["cache"][s0 + 1]
+                    keys[g, :, lanes] = jnp.concatenate([one[:, 0:HD], two[:, 0:HD]], axis=1)
+                    values[g, :, lanes] = jnp.concatenate([one[:, HD:], two[:, HD:]], axis=1)
+                else:
+                    keys[g, :, lanes] = jnp.zeros((block, LANES), BF16)
+                    values[g, :, lanes] = jnp.zeros((block, LANES), BF16)
+
     pass_on_from(1)
-    gate = silu(dot_nt(normed, ref["mi"][1]))
+    copies["cache"].wait()
+    third = quad_n // 3
+    pack(range(0, third))
     pass_on_from(2)
-    copies["wm"].wait()
-    memory = dot(normed, ref["wm"][...])
-    key_value = jnp.where(low8, rot(memory), memory).astype(BF16).astype(F32)
-    swapped = pltpu.roll(key_value, HD, 1)
-    key_both = jnp.where(low8, key_value, swapped)
-    value_both = jnp.where(low8, swapped, key_value)
-
-    own_score = []
-    for h in range(HEADS):
-        half = low8 if h % 2 == 0 else jnp.logical_not(low8)
-        prod = jnp.where(half, query[h // 2].astype(F32) * key_both, 0.0)
-        own_score.append(jnp.sum(prod, axis=1, keepdims=True) * HD**-0.5)
-
+    pack(range(third, 2 * third))
     pass_on_from(3)
+    pack(range(2 * third, quad_n))
     lane40 = lax.rem(lane8, SPAD)
     lane40 = jnp.where(lane8 < 3 * SPAD, lane40, -1)
     sr_row = jnp.full((ROWS, LANES), -1, jnp.int32)
@@ -226,6 +235,104 @@
 
     for distance in range(4, z_n // 2 + 1):
         pass_on_from(distance)
+    wait_all(q_all, 0, n - z_n, "recv")
+    q_sel = dot(own_pick, q_all[...].reshape(n * 8, 3 * LANES))
+    low40 = iota((SPAD, LANES), 1) < HD
+    for h in range(HEADS):
+        col = q_sel[:, (h // 2) * LANES : (h // 2 + 1) * LANES]
+        turn = pltpu.roll(col, HD, 1)
+        both = jnp.where(low40, col, turn) if h % 2 == 0 else jnp.where(low40, turn, col)
+        q_slot[h * SPAD : (h + 1) * SPAD, :] = both * HD**-0.5
+    time = iota((8, block), 1)
+
+    def live(s):
+        owner = ref["sr_s"][s]
+        used = owner >= 0
+        return jnp.where(used, ref["len_s"][jnp.where(used, owner, 0)] - ref["sb_s"][s] * block, 0)
+
+    zero = jnp.zeros((8, LANES), F32)
+    for g in range(quad_n):
+        lhs = []
+        for i in range(4):
+            q = q_slot[pl.ds(4 * g + i, 8, stride=SPAD), :]
+            q = jnp.where(low8, q, 0.0) if i % 2 == 0 else jnp.where(low8, 0.0, q)
+            lhs.append(jnp.concatenate([q, zero] if i < 2 else [zero, q], axis=1))
+        lhs = jnp.concatenate(lhs, axis=0).astype(BF16)
+        scores_v[g] = dot_nt(lhs, keys[g])
+    for g in range(quad_n):
+        for i in range(4):
+            s = 4 * g + i
+            rows = slice(i * 8, i * 8 + 8)
+            if s >= slots:
+                weights_v[g, rows, :] = jnp.zeros((8, block), BF16)
+                continue
+            scores = jnp.where(time < live(s), scores_v[g, rows, :], NEG)
+            top = jnp.max(scores, axis=1, keepdims=True)
+            weights = jnp.exp(scores - top).astype(BF16)
+            weights_v[g, rows, :] = weights
+            total = jnp.sum(weights.astype(F32), axis=1, keepdims=True)
+            stat_v[0, s] = jnp.broadcast_to(top + jnp.log(total), (8, LANES))
+            stat_v[1, s] = jnp.broadcast_to(1.0 / total, (8, LANES))
+    for g in range(quad_n):
+        out = dot(weights_v[g], values[g])
+        for i in range(4):
+            s = 4 * g + i
+            if s < slots:
+                part = out[i * 8 : i * 8 + 8, (i // 2) * LANES : (i // 2 + 1) * LANES] * stat_v[1, s]
+                lse = stat_v[0, s]
+                part = jnp.where(low8, part, lse) if i % 2 == 0 else jnp.where(low8, lse, part)
+                o_slot[pl.ds(s, 8, stride=SPAD), :] = part
+
+    lane40v = iota((SPAD, LANES), 1)
+    odd = (iota((SPAD, LANES), 0) & 1) == 1
+    outs, turned = [], []
+    for h in range(HEADS):
+        one = o_slot[h * SPAD : (h + 1) * SPAD, :]
+        two = pltpu.roll(one, HD, 1)
+        outs.append(jnp.where(odd, one, two))
+        turned.append(jnp.where(odd, two, one))
+    tail = jnp.where(lane40v == 80, ((sr_col & 7) + 1).astype(F32), 0.0)
+    for h in range(HEADS):
+        rest = turned[h]
+        for t in range(3):
+            term = rest.astype(BF16).astype(F32)
+            tail = jnp.where(lane40v == HD + 3 * h + t, term, tail)
+            rest = rest - term
+    table = jnp.concatenate(
+        [
+            jnp.where(low40, turned[0], outs[1]),
+            jnp.where(low40, turned[2], outs[3]),
+            jnp.where(low40, turned[4], tail),
+            jnp.zeros((8, LANES), F32),
+        ],
+        axis=0,
+    ).astype(BF16)
+    msg[...] = dot(pick, table).reshape(n, 8, LANES).astype(BF16)
+    inbox[me] = msg[me]
+
+    for i in list(reversed(z_order)) + [0]:
+        for j in reversed(range(plane_n)):
+            if i or j:
+                d = at(lax.rem(place + j, plane_n), lax.rem(z + i, z_n))
+                pltpu.make_async_remote_copy(
+                    src_ref=msg.at[d, pl.ds(0, 6)], dst_ref=inbox.at[me, pl.ds(0, 6)], send_sem=send_sem.at[3],
+                    recv_sem=recv_sem.at[3], device_id={"req": d},
+                ).start()
+
+    gate = silu(dot_nt(normed, ref["mi"][1]))
+    copies["wm"].wait()
+    memory = dot(normed, ref["wm"][...])
+    key_value = jnp.where(low8, rot(memory), memory).astype(BF16).astype(F32)
+    swapped = pltpu.roll(key_value, HD, 1)
+    key_both = jnp.where(low8, key_value, swapped)
+    value_both = jnp.where(low8, swapped, key_value)
+
+    own_score = []
+    for h in range(HEADS):
+        half = low8 if h % 2 == 0 else jnp.logical_not(low8)
+        prod = jnp.where(half, query[h // 2].astype(F32) * key_both, 0.0)
+        own_score.append(jnp.sum(prod, axis=1, keepdims=True) * HD**-0.5)
+
     wait_all(sel_buf, 1, tp_n - 1, "recv")
     selection = sel_buf[0]
     for p in range(1, tp_n):
@@ -270,91 +377,10 @@
     mamba_square = jnp.sum(mamba_y * mamba_y, axis=1, keepdims=True)
     share((mamba_y * ref["mg"][...]).astype(BF16), ref["mo"][...], mamba_square, m_send, m_recv, 2)
 
-    o_slot[...] = jnp.zeros_like(o_slot)
-    q_slot[...] = jnp.zeros_like(q_slot)
-    wait_all(q_all, 0, n - z_n, "recv")
-    q_sel = dot(own_pick, q_all[...].reshape(n * 8, 3 * LANES))
-    low40 = iota((SPAD, LANES), 1) < HD
-    for h in range(HEADS):
-        col = q_sel[:, (h // 2) * LANES : (h // 2 + 1) * LANES]
-        if h % 2 == 1:
-            col = pltpu.roll(col, HD, 1)
-        q_slot[h * SPAD : (h + 1) * SPAD, :] = jnp.where(low40, col, 0.0) * HD**-0.5
-    copies["cache"].wait()
-    block = ref["cache"].shape[1]
-    time = iota((16, block), 1)
-    first = iota((16, block), 0) < 8
-
-    def live(s):
-        owner = ref["sr_s"][s]
-        used = owner >= 0
-        return jnp.where(used, ref["len_s"][jnp.where(used, owner, 0)] - ref["sb_s"][s] * block, 0)
-
-    def attend(p, carry):
-        s0 = 2 * p
-        s1 = s0 + 1
-        pair = jnp.concatenate([ref["cache"][s0], ref["cache"][s1]], axis=1)
-        q0 = q_slot[pl.ds(s0, 8, stride=SPAD), :]
-        q1 = q_slot[pl.ds(s1, 8, stride=SPAD), :]
-        zero = jnp.zeros_like(q0)
-        lhs = jnp.concatenate(
-            [jnp.concatenate([q0, zero], axis=1), jnp.concatenate([zero, q1], axis=1)], axis=0
-        ).astype(BF16)
-        scores = dot_nt(lhs, pair)
-        ok = time < jnp.where(first, live(s0), live(s1))
-        scores = jnp.where(ok, scores, NEG)
-        top = jnp.max(scores, axis=1, keepdims=True)
-        weights = jnp.where(ok, jnp.exp(scores - top), 0.0).astype(BF16)
-        total = jnp.sum(weights.astype(F32), axis=1, keepdims=True)
-        total = jnp.where(total > 0.0, total, 1.0)
-        out = dot(weights, pair)
-        lse = top + jnp.log(total)
-        inv = 1.0 / total
-        o_slot[pl.ds(s0, 8, stride=SPAD), :] = jnp.where(low8, lse[0:8], out[0:8, 0:LANES] * inv[0:8])
-        o_slot[pl.ds(s1, 8, stride=SPAD), :] = jnp.where(low8, lse[8:16], out[8:16, LANES:] * inv[8:16])
-        return carry
-
-    lax.fori_loop(0, slots // 2, attend, 0, unroll=True)
-
-    lane40v = iota((SPAD, LANES), 1)
-    outs = [o_slot[h * SPAD : (h + 1) * SPAD, :] for h in range(HEADS)]
-    turned = [pltpu.roll(o, HD, 1) for o in outs]
-    tail = jnp.where(lane40v == 80, ((sr_col & 7) + 1).astype(F32), 0.0)
-    for h in range(HEADS):
-        rest = turned[h]
-        for t in range(3):
-            term = rest.astype(BF16).astype(F32)
-            tail = jnp.where(lane40v == HD + 3 * h + t, term, tail)
-            rest = rest - term
-    table = jnp.concatenate(
-        [
-            jnp.where(low40, turned[0], outs[1]),
-            jnp.where(low40, turned[2], outs[3]),
-            jnp.where(low40, turned[4], tail),
-            jnp.zeros((8, LANES), F32),
-        ],
-        axis=0,
-    ).astype(BF16)
-    msg[...] = dot(pick, table).reshape(n, 8, LANES).astype(BF16)
-    inbox[me] = msg[me]
-
-    def deliver(i, carry):
-        d = lax.rem(me + i, n)
-        pltpu.make_async_remote_copy(
-            src_ref=msg.at[d, pl.ds(0, 6)], dst_ref=inbox.at[me, pl.ds(0, 6)], send_sem=send_sem.at[3], recv_sem=recv_sem.at[3],
-            device_id={"req": d},
-        ).start()
-        return carry
-
-    lax.fori_loop(1, n, deliver, 0, unroll=7)
-
-    mamba = gathered(m_recv, 2)
-    mamba_scale = jnp.sqrt(mamba[:, TP_COLS : TP_COLS + 1] * (1.0 / (TP_COLS * tp_n)) + 1e-06)
     wide = jnp.concatenate([hidden, jnp.zeros((ROWS, 13 * LANES - width), F32)], axis=1)
     residual = wide[:, 0:TP_PAD]
     for p in range(1, tp_n):
         residual = jnp.where(tp == p, pltpu.roll(wide, wide.shape[1] - p * TP_COLS, 1)[:, 0:TP_PAD], residual)
-    base = residual + 0.5 * (mamba / mamba_scale)
     e_row = iota((16, LANES), 0)
     e_lane = iota((16, LANES), 1)
     e_start = HD + 3 * e_row
@@ -399,6 +425,9 @@
     )[:, 0 : HEADS * HD]
     attn_square = jnp.sum(attention * attention, axis=1, keepdims=True)
     share((attention * ref["ag"][...].reshape(1, HEADS * HD)).astype(BF16), ref["wo"][...], attn_square, a_send, a_recv, 4)
+    mamba = gathered(m_recv, 2)
+    mamba_scale = jnp.sqrt(mamba[:, TP_COLS : TP_COLS + 1] * (1.0 / (TP_COLS * tp_n)) + 1e-06)
+    base = residual + 0.5 * (mamba / mamba_scale)
     attn = gathered(a_recv, 4)
     attn_scale = jnp.sqrt(attn[:, TP_COLS : TP_COLS + 1] * (1.0 / (HEADS * HD * tp_n)) + 1e-06)
     final = base + 0.5 * (attn / attn_scale)
@@ -427,6 +456,7 @@
     n = lax.axis_size("req")
     tp_n = lax.axis_size("tp")
     slots, _, block, kv = cache_blocks.shape
+    quad_n = (slots + 3) // 4
     rate = 10000.0 ** (-(np.arange(LANES) % (HD // 2)) * (2.0 / HD))
     freq = jnp.asarray(np.broadcast_to(rate[None, :], (ROWS, LANES)), F32)
     row = lambda v: v.reshape(1, -1)
@@ -472,6 +502,11 @@
         pltpu.VMEM((8 * SPAD, LANES), F32),
         pltpu.VMEM((8 * SPAD, LANES), F32),
         pltpu.VMEM((ROWS, TP_COLS), F32),
+        pltpu.VMEM((quad_n, block, 2 * LANES), BF16),
+        pltpu.VMEM((quad_n, block, 2 * LANES), BF16),
+        pltpu.VMEM((quad_n, 32, block), F32),
+        pltpu.VMEM((quad_n, 32, block), BF16),
+        pltpu.VMEM((2, slots, 8, LANES), F32),
         pltpu.SemaphoreType.DMA((len(LOCAL),)),
         pltpu.SemaphoreType.DMA((5,)),
         pltpu.SemaphoreType.DMA((5,)),

time: 36.7 us -> 32.2 us (0.88)
  Pallas kernels: 36 us -> 31.4 us
    pallas_call x1, Pallas kernels: 35.3 us -> 30.7 us  [body(): pl.pallas_call(step, out_shape=(jax.ShapeDtypeStruct((ROWS, TP_COLS), BF1...]
where the time goes in v3:
time: 32.2 us; the launch traced here: 32.1 us
  Pallas kernels  31.4 us (98%)
  between operations  0.65 us (2%)
    pallas_call x1, Pallas kernels, body(): pl.pallas_call(step, out_shape=(jax.ShapeDtypeStruct((ROWS, TP_COLS), BF1...  30.7 us
    pallas_call x1, Pallas kernels, body(): pl.pallas_call(write_out, out_shape=results, in_specs=[pl.BlockSpec(memor...  0.72 us

profile of v3, /device:TPU:1, one launch (start us, length us, event | category | flops | bytes accessed | tf_op | source)
XLA Modules:
  0.0 32.1 jit_solution(10874718107421180025)
XLA Ops:
  0.6 30.7 %decode_layer.1 = (bf16[8,400]{1,0:T(8,128)(2,1)S(1)}, f32[8,16,400]{2,1,0:T(8,128)S(1)}) custom-call(s32[512]{0:T(512)} %refs_0_.1, s32[34]{0:T(128)} %refs_1_.1, s32[34]{0:T(128)} %refs_2_.1, bf16[8,1600]{1,0:T(8,128)(2,1)} %refs_3_.1, f32[1600]{0:T(1024)} %refs_4_.1, f32[8,128]{1,0:T(8,128)} %constant.2.clone.refs_5_, bf16[320,1600]{1,0:T(8,128)(2,1)} %bitcast.11, ...), custom_call_target="tpu_custom_call" | custom-call | tf_op jit(solution)/shard_map/decode_layer/pallas_call | solution.py:519
  31.4 0.7 %write_out.1 = (bf16[8,400]{1,0:T(8,128)(2,1)}, f32[8,16,400]{2,1,0:T(8,128)}) custom-call(bf16[8,400]{1,0:T(8,128)(2,1)S(1)} %get-tuple-element.4.layer, f32[8,16,400]{2,1,0:T(8,128)S(1)} %get-tuple-element.5.state), custom_call_target="tpu_custom_call" | custom-call | tf_op jit(solution)/shard_map/write_out/pallas_call | solution.py:532

commit v4 on v3

--- a/solution.py
+++ b/solution.py
@@ -58,38 +58,45 @@
     ref = dict(zip(LOCAL, refs[: len(LOCAL)]))
     (
         q_all, sel_buf, msg, inbox, m_send, m_recv, a_send, a_recv, q_slot, o_slot, y_v,
-        keys, values, scores_v, weights_v, stat_v,
+        keys, values, scores_v, weights_v, stat_v, pick,
         in_sem, send_sem, recv_sem, z_sem,
     ) = refs[len(LOCAL) :]
     me = lax.axis_index("req")
     tp = lax.axis_index("tp")
 
+    z_n = depth_of(n)
+    plane_n = n // z_n
+    x_n = plane_n // 2
+    core = lax.rem(me, 2)
+    z = lax.rem(lax.div(me, 2), z_n)
+    x = lax.div(me, 2 * z_n)
+
+    def ahead(at, by, count, stride):
+        return jnp.where(at >= count - by, (by - count) * stride, by * stride) if by else 0
+
+    z_order = sorted(range(1, z_n), key=lambda i: (min(i, z_n - i), i))
+    z_step = {i: ahead(z, i, z_n, 2) for i in range(z_n)}
+    column = {i: me + z_step[i] for i in z_order}
+    x_step = {i: ahead(x, i, x_n, 2 * z_n) for i in range(x_n)}
+    core_step = {0: 0, 1: 1 - 2 * core}
+    plane_order = sorted(range(1, plane_n), key=lambda j: -min(j // 2, x_n - j // 2))
+    plane_step = [x_step[j // 2] + core_step[j % 2] for j in plane_order]
+    plane = [me + step for step in plane_step]
+    tp_peer = [tp + ahead(tp, i, tp_n, 1) for i in sorted(range(1, tp_n), key=lambda i: -min(i, tp_n - i))]
+
+    barrier = pltpu.get_barrier_semaphore()
+    for i in reversed(z_order):
+        pl.semaphore_signal(barrier, inc=1, device_id={"req": column[i]})
+    for d in plane:
+        pl.semaphore_signal(barrier, inc=1, device_id={"req": d})
+    for p in tp_peer:
+        pl.semaphore_signal(barrier, inc=1, device_id={"tp": p})
     copies = {}
     for k, name in enumerate(LOCAL):
         dst = ref[name].at[pl.ds(0, HEADS * HD)] if name == "wq" else ref[name]
         copies[name] = pltpu.make_async_copy(hbm[name], dst, in_sem.at[k])
         copies[name].start()
 
-    z_n = depth_of(n)
-    plane_n = n // z_n
-    core = lax.rem(me, 2)
-    z = lax.rem(me // 2, z_n)
-    place = me // (2 * z_n) * 2 + core
-
-    def at(place, z):
-        return place // 2 * (2 * z_n) + z * 2 + lax.rem(place, 2)
-
-    z_order = sorted(range(1, z_n), key=lambda i: (min(i, z_n - i), i))
-    column = {i: at(place, lax.rem(z + i, z_n)) for i in z_order}
-    plane = [at(lax.rem(place + j, plane_n), z) for j in range(1, plane_n)]
-
-    barrier = pltpu.get_barrier_semaphore()
-    for i in reversed(z_order):
-        pl.semaphore_signal(barrier, inc=1, device_id={"req": column[i]})
-    for d in plane:
-        pl.semaphore_signal(barrier, inc=1, device_id={"req": d})
-    for i in range(1, tp_n):
-        pl.semaphore_signal(barrier, inc=1, device_id={"tp": lax.rem(tp + i, tp_n)})
     inbox[...] = jnp.zeros_like(inbox)
     o_slot[...] = jnp.zeros_like(o_slot)
     q_slot[...] = jnp.zeros_like(q_slot)
@@ -97,8 +104,7 @@
     quad_n = (slots + 3) // 4
 
     def tp_start(src, dst, k):
-        for i in range(1, tp_n):
-            p = lax.rem(tp + i, tp_n)
+        for p in tp_peer:
             pltpu.make_async_remote_copy(
                 src_ref=src(p), dst_ref=dst.at[tp], send_sem=send_sem.at[k], recv_sem=recv_sem.at[k],
                 device_id={"tp": p},
@@ -164,7 +170,7 @@
     def pass_on_from(distance):
         for i in z_order:
             if min(i, z_n - i) == distance:
-                source = at(place, lax.rem(z + z_n - i, z_n))
+                source = column[z_n - i]
                 z_copy(i, source, source).wait_recv()
                 pass_on(source)
 
@@ -202,10 +208,9 @@
     copies["cache"].wait()
     third = quad_n // 3
     pack(range(0, third))
-    pass_on_from(2)
-    pack(range(third, 2 * third))
-    pass_on_from(3)
-    pack(range(2 * third, quad_n))
+    for distance in range(2, z_n // 2 + 1):
+        pass_on_from(distance)
+    pack(range(third, quad_n))
     lane40 = lax.rem(lane8, SPAD)
     lane40 = jnp.where(lane8 < 3 * SPAD, lane40, -1)
     sr_row = jnp.full((ROWS, LANES), -1, jnp.int32)
@@ -220,21 +225,15 @@
     for s in range(slots):
         d = lax.shift_right_arithmetic(ref["sr_s"][s], 3)
         rank_row = rank_row + jnp.where((dest_row == d) & (lane40 > s), 1, 0)
-    m_rows = n * 8
-    mr = iota((m_rows, LANES), 0)
-    mj = lax.shift_right_arithmetic(mr & 7, 1)
+    mr = iota((8, LANES), 0)
     cj = jnp.where(lane8 < SPAD, 0, jnp.where(lane8 < 2 * SPAD, 1, jnp.where(lane8 < 3 * SPAD, 2, -1)))
-    pick = (
-        (lax.shift_right_arithmetic(mr, 3) == dest_row[0:1, :])
-        & ((mr & 1) == rank_row[0:1, :])
-        & (mj == cj[0:1, :])
-    )
-    pick = jnp.where(pick, 1.0, 0.0).astype(BF16)
+    fits = ((mr & 1) == rank_row) & (lax.shift_right_arithmetic(mr, 1) == cj)
+    dests = [me + (z_step[i] + step) for i in list(reversed(z_order)) + [0] for step in plane_step + [0]]
+    for k, d in enumerate(dests):
+        pick[k * 8 : (k + 1) * 8, :] = jnp.where(fits & (dest_row == d), 1.0, 0.0)
     own_pick = jnp.concatenate([sr_col] * (n * 8 // LANES), axis=1) if n * 8 >= LANES else sr_col[:, 0 : n * 8]
     own_pick = jnp.where(own_pick == iota((SPAD, n * 8), 1), 1.0, 0.0).astype(BF16)
 
-    for distance in range(4, z_n // 2 + 1):
-        pass_on_from(distance)
     wait_all(q_all, 0, n - z_n, "recv")
     q_sel = dot(own_pick, q_all[...].reshape(n * 8, 3 * LANES))
     low40 = iota((SPAD, LANES), 1) < HD
@@ -307,17 +306,16 @@
         ],
         axis=0,
     ).astype(BF16)
-    msg[...] = dot(pick, table).reshape(n, 8, LANES).astype(BF16)
-    inbox[me] = msg[me]
-
-    for i in list(reversed(z_order)) + [0]:
-        for j in reversed(range(plane_n)):
-            if i or j:
-                d = at(lax.rem(place + j, plane_n), lax.rem(z + i, z_n))
-                pltpu.make_async_remote_copy(
-                    src_ref=msg.at[d, pl.ds(0, 6)], dst_ref=inbox.at[me, pl.ds(0, 6)], send_sem=send_sem.at[3],
-                    recv_sem=recv_sem.at[3], device_id={"req": d},
-                ).start()
+    part_n = n // 4
+    for c in range(4):
+        rows = pick[c * part_n * 8 : (c + 1) * part_n * 8, :].astype(BF16)
+        msg[c * part_n : (c + 1) * part_n] = dot(rows, table).reshape(part_n, 8, LANES).astype(BF16)
+        for k in range(c * part_n, min((c + 1) * part_n, n - 1)):
+            pltpu.make_async_remote_copy(
+                src_ref=msg.at[k, pl.ds(0, 6)], dst_ref=inbox.at[me, pl.ds(0, 6)], send_sem=send_sem.at[3],
+                recv_sem=recv_sem.at[3], device_id={"req": dests[k]},
+            ).start()
+    inbox[me] = msg[n - 1]
 
     gate = silu(dot_nt(normed, ref["mi"][1]))
     copies["wm"].wait()
@@ -360,19 +358,27 @@
         proj = dot(used, weight)
         extra = jnp.zeros((ROWS, 13 * LANES - proj.shape[1]), F32)
         proj = jnp.concatenate([proj, extra], axis=1)
-        tail = iota((ROWS, TP_PAD), 1) >= TP_COLS
+        lane = iota((ROWS, TP_PAD), 1)
+        terms, remain = jnp.zeros((ROWS, TP_PAD), F32), square
+        for k_term in range(3):
+            term = remain.astype(BF16).astype(F32)
+            terms = jnp.where(lane == TP_COLS + k_term, term, terms)
+            remain = remain - term
         for p in range(tp_n):
             moved = proj if p == 0 else pltpu.roll(proj, proj.shape[1] - p * TP_COLS, 1)
-            send[p] = jnp.where(tail, square, moved[:, 0:TP_PAD])
+            send[p] = jnp.where(lane >= TP_COLS, terms, moved[:, 0:TP_PAD]).astype(send.dtype)
         recv[tp] = send[tp]
         tp_start(lambda p: send.at[p], recv, k)
 
     def gathered(recv, k):
         wait_all(recv, k, tp_n - 1, "recv")
-        total = recv[0]
+        total = recv[0].astype(F32)
         for p in range(1, tp_n):
-            total = total + recv[p]
-        return total
+            total = total + recv[p].astype(F32)
+        square = total[:, TP_COLS : TP_COLS + 1]
+        for k_term in range(1, 3):
+            square = square + total[:, TP_COLS + k_term : TP_COLS + k_term + 1]
+        return total, square
 
     mamba_square = jnp.sum(mamba_y * mamba_y, axis=1, keepdims=True)
     share((mamba_y * ref["mg"][...]).astype(BF16), ref["mo"][...], mamba_square, m_send, m_recv, 2)
@@ -425,11 +431,11 @@
     )[:, 0 : HEADS * HD]
     attn_square = jnp.sum(attention * attention, axis=1, keepdims=True)
     share((attention * ref["ag"][...].reshape(1, HEADS * HD)).astype(BF16), ref["wo"][...], attn_square, a_send, a_recv, 4)
-    mamba = gathered(m_recv, 2)
-    mamba_scale = jnp.sqrt(mamba[:, TP_COLS : TP_COLS + 1] * (1.0 / (TP_COLS * tp_n)) + 1e-06)
+    mamba, square = gathered(m_recv, 2)
+    mamba_scale = jnp.sqrt(square * (1.0 / (TP_COLS * tp_n)) + 1e-06)
     base = residual + 0.5 * (mamba / mamba_scale)
-    attn = gathered(a_recv, 4)
-    attn_scale = jnp.sqrt(attn[:, TP_COLS : TP_COLS + 1] * (1.0 / (HEADS * HD * tp_n)) + 1e-06)
+    attn, square = gathered(a_recv, 4)
+    attn_scale = jnp.sqrt(square * (1.0 / (HEADS * HD * tp_n)) + 1e-06)
     final = base + 0.5 * (attn / attn_scale)
     out_layer[...] = final[:, 0:TP_COLS].astype(BF16)
     wait_all(q_all, 0, n - 1, "send")
@@ -507,6 +513,7 @@
         pltpu.VMEM((quad_n, 32, block), F32),
         pltpu.VMEM((quad_n, 32, block), BF16),
         pltpu.VMEM((2, slots, 8, LANES), F32),
+        pltpu.VMEM((n * 8, LANES), F32),
         pltpu.SemaphoreType.DMA((len(LOCAL),)),
         pltpu.SemaphoreType.DMA((5,)),
         pltpu.SemaphoreType.DMA((5,)),

time: 32.2 us -> 31.9 us (level)
  no operation moved by 1% of the time
where the time goes in v4:
time: 31.9 us
  Pallas kernels  31.2 us (98%)
  between operations  0.65 us (2%)
    pallas_call x1, Pallas kernels, body(): pl.pallas_call(step, out_shape=(jax.ShapeDtypeStruct((ROWS, TP_COLS), BF1...  30.5 us
    pallas_call x1, Pallas kernels, body(): pl.pallas_call(write_out, out_shape=results, in_specs=[pl.BlockSpec(memor...  0.72 us

profile of v4, /device:TPU:1, one launch (start us, length us, event | category | flops | bytes accessed | tf_op | source)
XLA Modules:
  0.0 31.9 jit_solution(3978095487349743030)
XLA Ops:
  0.6 30.5 %decode_layer.1 = (bf16[8,400]{1,0:T(8,128)(2,1)S(1)}, f32[8,16,400]{2,1,0:T(8,128)S(1)}) custom-call(s32[512]{0:T(512)} %refs_0_.1, s32[34]{0:T(128)} %refs_1_.1, s32[34]{0:T(128)} %refs_2_.1, bf16[8,1600]{1,0:T(8,128)(2,1)} %refs_3_.1, f32[1600]{0:T(1024)} %refs_4_.1, f32[8,128]{1,0:T(8,128)} %constant.2.clone.refs_5_, bf16[320,1600]{1,0:T(8,128)(2,1)} %bitcast.11, ...), custom_call_target="tpu_custom_call" | custom-call | tf_op jit(solution)/shard_map/decode_layer/pallas_call | solution.py:526
  31.1 0.7 %write_out.1 = (bf16[8,400]{1,0:T(8,128)(2,1)}, f32[8,16,400]{2,1,0:T(8,128)}) custom-call(bf16[8,400]{1,0:T(8,128)(2,1)S(1)} %get-tuple-element.4.layer, f32[8,16,400]{2,1,0:T(8,128)S(1)} %get-tuple-element.5.state), custom_call_target="tpu_custom_call" | custom-call | tf_op jit(solution)/shard_map/write_out/pallas_call | solution.py:539

commit v5 on v4

--- a/solution.py
+++ b/solution.py
@@ -200,9 +200,6 @@
                     one, two = ref["cache"][s0], ref["cache"][s0 + 1]
                     keys[g, :, lanes] = jnp.concatenate([one[:, 0:HD], two[:, 0:HD]], axis=1)
                     values[g, :, lanes] = jnp.concatenate([one[:, HD:], two[:, HD:]], axis=1)
-                else:
-                    keys[g, :, lanes] = jnp.zeros((block, LANES), BF16)
-                    values[g, :, lanes] = jnp.zeros((block, LANES), BF16)
 
     pass_on_from(1)
     copies["cache"].wait()
@@ -251,19 +248,19 @@
 
     zero = jnp.zeros((8, LANES), F32)
     for g in range(quad_n):
+        held = min(4, slots - 4 * g)
         lhs = []
-        for i in range(4):
+        for i in range(held):
             q = q_slot[pl.ds(4 * g + i, 8, stride=SPAD), :]
             q = jnp.where(low8, q, 0.0) if i % 2 == 0 else jnp.where(low8, 0.0, q)
-            lhs.append(jnp.concatenate([q, zero] if i < 2 else [zero, q], axis=1))
+            lhs.append(q if held == 2 else jnp.concatenate([q, zero] if i < 2 else [zero, q], axis=1))
         lhs = jnp.concatenate(lhs, axis=0).astype(BF16)
-        scores_v[g] = dot_nt(lhs, keys[g])
+        scores_v[g, 0 : 8 * held, :] = dot_nt(lhs, keys[g, :, 0 : HD * held])
     for g in range(quad_n):
         for i in range(4):
             s = 4 * g + i
             rows = slice(i * 8, i * 8 + 8)
             if s >= slots:
-                weights_v[g, rows, :] = jnp.zeros((8, block), BF16)
                 continue
             scores = jnp.where(time < live(s), scores_v[g, rows, :], NEG)
             top = jnp.max(scores, axis=1, keepdims=True)
@@ -273,7 +270,8 @@
             stat_v[0, s] = jnp.broadcast_to(top + jnp.log(total), (8, LANES))
             stat_v[1, s] = jnp.broadcast_to(1.0 / total, (8, LANES))
     for g in range(quad_n):
-        out = dot(weights_v[g], values[g])
+        held = min(4, slots - 4 * g)
+        out = dot(weights_v[g, 0 : 8 * held, :], values[g, :, 0 : HD * held])
         for i in range(4):
             s = 4 * g + i
             if s < slots:

time: 31.9 us -> 31.8 us (level)
  no operation moved by 1% of the time
where the time goes in v5:
time: 31.8 us
  Pallas kernels  31.1 us (98%)
  between operations  0.65 us (2%)
    pallas_call x1, Pallas kernels, body(): pl.pallas_call(step, out_shape=(jax.ShapeDtypeStruct((ROWS, TP_COLS), BF1...  30.4 us
    pallas_call x1, Pallas kernels, body(): pl.pallas_call(write_out, out_shape=results, in_specs=[pl.BlockSpec(memor...  0.72 us

profile of v5, /device:TPU:1, one launch (start us, length us, event | category | flops | bytes accessed | tf_op | source)
XLA Modules:
  0.0 31.8 jit_solution(281127151145153606)
XLA Ops:
  0.6 30.4 %decode_layer.1 = (bf16[8,400]{1,0:T(8,128)(2,1)S(1)}, f32[8,16,400]{2,1,0:T(8,128)S(1)}) custom-call(s32[512]{0:T(512)} %refs_0_.1, s32[34]{0:T(128)} %refs_1_.1, s32[34]{0:T(128)} %refs_2_.1, bf16[8,1600]{1,0:T(8,128)(2,1)} %refs_3_.1, f32[1600]{0:T(1024)} %refs_4_.1, f32[8,128]{1,0:T(8,128)} %constant.2.clone.refs_5_, bf16[320,1600]{1,0:T(8,128)(2,1)} %bitcast.11, ...), custom_call_target="tpu_custom_call" | custom-call | tf_op jit(solution)/shard_map/decode_layer/pallas_call | solution.py:524
  31.0 0.7 %write_out.1 = (bf16[8,400]{1,0:T(8,128)(2,1)}, f32[8,16,400]{2,1,0:T(8,128)}) custom-call(bf16[8,400]{1,0:T(8,128)(2,1)S(1)} %get-tuple-element.4.layer, f32[8,16,400]{2,1,0:T(8,128)S(1)} %get-tuple-element.5.state), custom_call_target="tpu_custom_call" | custom-call | tf_op jit(solution)/shard_map/write_out/pallas_call | solution.py:537
